TPU v7x, 256 devices: a whole 4x4x8 slice. The times are simulated.
256 devices in a mesh: loop: 32 (over z, x_lo, core), tok: 8 (over y, x_hi).
Axes of the slice: x: 4 (x_hi: 2, x_lo: 2; x = x_hi * 2 + x_lo), y: 4, z: 8, core: 2. Of those that a mesh axis runs over, the one named last changes fastest.
Arguments:
- features: bfloat16 [4096, 4096], P('loop', 'tok'), may hold values from -6 to 6
- expert_rows: int32 [2, 768], replicated, may hold values from 0 to 4095, as said below
- route_weight: float32 [2, 768], replicated, may hold values from 0.1 to 1
- gate_proj: bfloat16 [2, 4096, 14336], P(None, 'tok', 'loop'), may hold values from -0.09375 to 0.09375
- up_proj: bfloat16 [2, 4096, 14336], P(None, 'tok', 'loop'), may hold values from -0.09375 to 0.09375
- down_proj: bfloat16 [2, 14336, 4096], P(None, 'loop', 'tok'), may hold values from -0.046875 to 0.046875
- out_grad: bfloat16 [4096, 4096], P('loop', 'tok'), may hold values from -6 to 6
Outputs:
- mixed: bfloat16 [4096, 4096], P('loop', 'tok')
- feature_grad: bfloat16 [4096, 4096], P('loop', 'tok')
- gate_grad: bfloat16 [2, 4096, 14336], P(None, 'tok', 'loop')
- up_grad: bfloat16 [2, 4096, 14336], P(None, 'tok', 'loop')
- down_grad: bfloat16 [2, 14336, 4096], P(None, 'loop', 'tok')
Inputs may be any that keep to these rules, and one draw needn't show every extreme that they name: `expert_rows`: each expert's list holds 768 distinct tokens in ascending order, and tokens 0 and 4095 are in every list. Of the 128 tokens t with the same t // 128, at most 48 are in one list, and in every list exactly 48 come from one such index.
All inputs are finite; a program needn't handle non-finite values.
Results may differ from a plain program's by a relative error of at most 0.0049.
Values may be sent and summed in bfloat16 or wider, within the bound.
A program may use at most 128 MiB of HBM per device.

v0:
```python
import jax
import jax.numpy as jnp
from jax import lax
from jax.sharding import PartitionSpec as P


def local_grads(back, weights, gate, upval):
    weighted = weights[:, :, None] * back
    sigma = jax.nn.sigmoid(gate)
    gate_bar = (weighted * upval * sigma * (1.0 + gate * (1.0 - sigma))).astype(jnp.bfloat16)
    up_bar = (weighted * gate * sigma).astype(jnp.bfloat16)
    return (gate_bar, up_bar)


def local(features, expert_rows, route_weight, gate_proj, up_proj, down_proj, out_grad):
    loop_size = lax.axis_size("loop")
    local_tokens = features.shape[0]
    width = features.shape[1]
    total_tokens = local_tokens * loop_size
    flat_rows = expert_rows.reshape(-1)
    everyone = lax.all_gather(features, "loop", axis=0, tiled=True)
    token_rows = everyone[expert_rows]
    gate_part = jnp.einsum(
        "erd,edf->erf", token_rows, gate_proj, preferred_element_type=jnp.float32
    )
    up_part = jnp.einsum("erd,edf->erf", token_rows, up_proj, preferred_element_type=jnp.float32)
    gate_full, up_full = lax.psum((gate_part, up_part), "tok")
    scaled = (route_weight[:, :, None] * jax.nn.silu(gate_full) * up_full).astype(jnp.bfloat16)
    expert_out = jnp.einsum("erf,efd->erd", scaled, down_proj, preferred_element_type=jnp.float32)
    out_buffer = (
        jnp.zeros((total_tokens, width), jnp.float32)
        .at[flat_rows]
        .add(expert_out.reshape(-1, width))
    )
    mixed = lax.psum_scatter(out_buffer, "loop", scatter_dimension=0, tiled=True).astype(
        jnp.bfloat16
    )
    grad_everyone = lax.all_gather(out_grad, "loop", axis=0, tiled=True)
    grad_rows = grad_everyone[expert_rows]
    back_part = jnp.einsum("erd,efd->erf", grad_rows, down_proj, preferred_element_type=jnp.float32)
    back_full = lax.psum(back_part, "tok")
    gate_bar, up_bar = local_grads(back_full, route_weight, gate_full, up_full)
    input_part = jnp.einsum("erf,edf->erd", gate_bar, gate_proj, preferred_element_type=jnp.float32)
    input_part = input_part + jnp.einsum(
        "erf,edf->erd", up_bar, up_proj, preferred_element_type=jnp.float32
    )
    grad_buffer = (
        jnp.zeros((total_tokens, width), jnp.float32)
        .at[flat_rows]
        .add(input_part.reshape(-1, width))
    )
    feature_grad = lax.psum_scatter(grad_buffer, "loop", scatter_dimension=0, tiled=True).astype(
        jnp.bfloat16
    )
    gate_grad = jnp.einsum(
        "erd,erf->edf", token_rows, gate_bar, preferred_element_type=jnp.float32
    ).astype(jnp.bfloat16)
    up_grad = jnp.einsum(
        "erd,erf->edf", token_rows, up_bar, preferred_element_type=jnp.float32
    ).astype(jnp.bfloat16)
    down_grad = jnp.einsum(
        "erf,erd->efd", scaled, grad_rows, preferred_element_type=jnp.float32
    ).astype(jnp.bfloat16)
    return (mixed, feature_grad, gate_grad, up_grad, down_grad)


def solution(mesh):
    placed = (
        P("loop", "tok"),
        P(),
        P(),
        P(None, "tok", "loop"),
        P(None, "tok", "loop"),
        P(None, "loop", "tok"),
        P("loop", "tok"),
    )
    return jax.shard_map(
        local,
        mesh=mesh,
        in_specs=placed,
        out_specs=(
            P("loop", "tok"),
            P("loop", "tok"),
            P(None, "tok", "loop"),
            P(None, "tok", "loop"),
            P(None, "loop", "tok"),
        ),
        check_vma=False,
    )
```

profile of v0, /device:TPU:1, one launch (start us, length us, event | category | flops | bytes accessed | tf_op | source)
XLA Modules:
  0.0 795.2 jit_solution(1606482351120809386)
XLA Ops:
  7.2 0.0 copy-start
  7.2 0.0 all-gather.3.cloned.1.call-start
  7.2 0.7 all-gather.3.cloned.1.call-update
  7.9 0.0 all-gather.5.cloned.1.call-start
  8.0 0.7 all-gather.5.cloned.1.call-update
  8.7 0.0 all-reduce.3.cloned.1.call-start
  8.7 0.7 compare_select_fusion.1
  9.4 71.1 %all-gather.3.cloned.1.call-done = bf16[4096,512]{1,0:T(8,128)(2,1)} async-done(((bf16[128,512]{1,0:T(8,128)(2,1)}), bf16[4096,512]{1,0:T(8,128)(2,1)}) %all-gather.3.cloned.1.call-update) | async-done | bytes 4194320 | tf_op jit(solution)/shard_map/all_gather | solution.py:21
  80.6 7.6 gather_fusion
  88.2 0.0 copy-start.6
  88.2 0.0 copy-done
  88.2 2.5 fusion.5
  90.7 0.0 copy-done.6
  90.7 2.5 fusion.6
  93.2 55.7 %all-gather.5.cloned.1.call-done = bf16[4096,512]{1,0:T(8,128)(2,1)} async-done(((bf16[128,512]{1,0:T(8,128)(2,1)}), bf16[4096,512]{1,0:T(8,128)(2,1)}) %all-gather.5.cloned.1.call-update) | async-done | bytes 4194320 | tf_op jit(solution)/shard_map/all_gather | solution.py:38
  148.9 8.2 %gather_fusion.1 = bf16[1536,512]{1,0:T(8,128)(2,1)} fusion(bf16[4096,512]{1,0:T(8,128)(2,1)} %all-gather.5.cloned.1.call-done, s32[2048]{0:T(1024)S(1)} %pad_clamp_fusion), kind=kCustom, calls=%fused_computation.1 | custom fusion | bytes 3151872 | tf_op jit(solution)/shard_map/gather | solution.py:39
  157.1 4.1 fusion.8
  161.2 0.0 copy-start.8
  161.2 0.0 copy-start.9
  161.2 0.0 all-reduce.3.cloned.1.call-update
  161.2 0.0 reduce-scatter.5.cloned.1.call-start
  161.3 0.6 copy-done.8
  161.9 340.6 %all-reduce.3.cloned.1.call-done = (f32[2,768,448]{1,2,0:T(8,128)}, f32[2,768,448]{1,2,0:T(8,128)}, f32[2,768,448]{1,2,0:T(8,128)}) async-done(((f32[2,768,448]{1,2,0:T(8,128)}, f32[2,768,448]{1,2,0:T(8,128)}, f32[2,768,448]{1,2,0:T(8,128)}), (f32[2,768,448]{1,2,0:T(8,128)}, f32[2,768,448]{1,2,0:T(8,128)}, f32[2,768,448]{1,2,0:T(8,128)})) %all-reduce.3.cloned.1.call-update) | async-done | bytes 8257552 | tf_op jit(solution)/shard_map/psum | solution.py:27
  502.5 0.0 copy-done.9
  502.5 5.2 multiply_convert_fusion
  507.7 0.0 copy-start.3
  507.7 0.0 copy-start.5
  507.7 1.0 fusion.9
  508.7 2.8 convolution_add_fusion
  511.5 0.0 copy-done.3
  511.5 0.0 copy-done.5
  511.5 14.0 %scatter_custom_fusion.1 = f32[4096,512]{1,0:T(8,128)} fusion(s32[1536]{0:T(1024)S(1)} %fusion.4, f32[1536,512]{1,0:T(8,128)} %bitcast.32, f32[]{:T(128)} %constant.4.clone.1), kind=kCustom, calls=%fused_computation.4 | custom fusion | flops 786432 | bytes 8389120 | tf_op jit(solution)/shard_map/scatter-add | solution.py:50
  525.5 0.0 copy-start.7
  525.5 0.0 reduce-scatter.5.cloned.1.call-update
  525.5 0.0 reduce-scatter.3.cloned.1.call-start
  525.5 1.1 copy-done.7
  526.6 4.0 fusion.7
  530.6 14.0 %scatter_custom_fusion = f32[4096,512]{1,0:T(8,128)} fusion(s32[1536]{0:T(1024)S(1)} %fusion.4, f32[1536,512]{1,0:T(8,128)} %bitcast.33, f32[]{:T(128)} %constant.4.clone.1), kind=kCustom, calls=%fused_computation.6 | custom fusion | flops 786432 | bytes 8389120 | tf_op jit(solution)/shard_map/scatter-add | solution.py:33
  544.6 0.0 reduce-scatter.3.cloned.1.call-update
  544.6 0.0 copy-start.4
  544.6 3.3 convolution_convert_fusion
  547.9 0.0 copy-done.4
  547.9 0.0 copy-start.1
  547.9 0.0 copy-start.2
  547.9 1.8 convolution_convert_fusion.1
  549.7 0.0 copy-done.1
  549.7 0.1 copy-done.2
  549.8 1.8 convolution_convert_fusion.2
  551.6 102.9 %reduce-scatter.5.cloned.1.call-done = f32[128,512]{1,0:T(8,128)} async-done(((f32[4096,512]{1,0:T(8,128)}), f32[128,512]{1,0:T(8,128)}) %reduce-scatter.5.cloned.1.call-update) | async-done | bytes 262160 | tf_op jit(solution)/shard_map/reduce_scatter | solution.py:52
  654.5 1.6 convert_element_type.28
  656.2 130.9 %reduce-scatter.3.cloned.1.call-done = f32[128,512]{1,0:T(8,128)} async-done(((f32[4096,512]{1,0:T(8,128)}), f32[128,512]{1,0:T(8,128)}) %reduce-scatter.3.cloned.1.call-update) | async-done | bytes 262160 | tf_op jit(solution)/shard_map/reduce_scatter | solution.py:35
  787.1 1.6 convert_element_type.25
  (4 shorter events, 0.1 us)
Async XLA Ops:
  7.2 81.0 %copy-start = (bf16[2,512,448]{1,2,0:T(8,128)(2,1)S(1)}, bf16[2,512,448]{1,2,0:T(8,128)(2,1)}, u32[]{:S(2)}) copy-start(bf16[2,512,448]{1,2,0:T(8,128)(2,1)} %param.10) | copy-start | bytes 2752516
  7.2 73.4 %all-gather.3.cloned.1.call-start = ((), (), s32[]{:S(2)}) async-start(), calls=%async_computation.2 | async-start | bytes 4325376 | tf_op jit(solution)/shard_map/all_gather | solution.py:21
  7.9 141.0 %all-gather.5.cloned.1.call-start = ((), (), s32[]{:S(2)}) async-start(), calls=%async_computation.4 | async-start | bytes 4325376 | tf_op jit(solution)/shard_map/all_gather | solution.py:38
  8.7 493.9 %all-reduce.3.cloned.1.call-start = ((), (), s32[]{:S(2)}) async-start(), calls=%async_computation.6 | async-start | bytes 16515072 | tf_op jit(solution)/shard_map/psum | solution.py:27
  88.2 2.6 copy-start.6
  161.2 0.7 copy-start.8
  161.2 341.3 %copy-start.9 = (f32[2,768]{1,0:T(2,128)S(1)}, f32[2,768]{1,0:T(2,128)}, u32[]{:S(2)}) copy-start(f32[2,768]{1,0:T(2,128)} %param.9) | copy-start | bytes 18436
  161.2 493.3 %reduce-scatter.5.cloned.1.call-start = ((), (), s32[]{:S(2)}) async-start(), calls=%async_computation.5 | async-start | bytes 8650752 | tf_op jit(solution)/shard_map/reduce_scatter | solution.py:52
  507.7 3.8 copy-start.3
  507.7 3.8 copy-start.5
  525.5 1.2 copy-start.7
  525.5 261.6 %reduce-scatter.3.cloned.1.call-start = ((), (), s32[]{:S(2)}) async-start(), calls=%async_computation.3 | async-start | bytes 8650752 | tf_op jit(solution)/shard_map/reduce_scatter | solution.py:35
  544.6 3.3 copy-start.4
  547.9 1.8 copy-start.1
  547.9 1.9 copy-start.2
Sparse Core Ops, SparseCore 0:
  9.8 70.6 all-gather.2
  82.4 66.4 all-gather.4
  161.3 341.1 all-reduce.2
  525.6 128.8 reduce-scatter.4
  656.9 130.0 reduce-scatter.2
where the time goes:
time: 798 us; the launch traced here: 795 us
  waiting for transfers between devices  703 us (88%)
  other arithmetic  37.1 us (5%)
  matrix products  23.7 us (3%)
  local copies, waits for them, and re-layouts  17.7 us (2%)
  between operations  13.8 us (2%)
    psum x1, waiting for transfers between devices, local(): gate_full, up_full = lax.psum((gate_part, up_part), 'tok')  341 us
    reduce_scatter x1, waiting for transfers between devices, local(): lax.psum_scatter(out_buffer, 'loop', scatter_dimension=0, tiled=True)  131 us
    reduce_scatter x1, waiting for transfers between devices, local(): lax.psum_scatter(grad_buffer, 'loop', scatter_dimension=0, tiled=True)  103 us
    all_gather x1, waiting for transfers between devices, local(): everyone = lax.all_gather(features, 'loop', axis=0, tiled=True)  71.1 us
    all_gather x1, waiting for transfers between devices, local(): grad_everyone = lax.all_gather(out_grad, 'loop', axis=0, tiled=True)  55.7 us
  transfers between devices with their start and end apart: 5, of which 5 were waited for; matrix products, arithmetic and copies ran while one was open for 5% of the time, Pallas kernels for 0%

commit v1 on v0

v1 whole, which is shorter than its diff:
```python
import jax
import jax.numpy as jnp
from jax import lax
from jax.sharding import PartitionSpec as P

SLOTS = 48


def dot(a, b, ca, cb, dtype=jnp.float32):
    return lax.dot_general(a, b, (((ca,), (cb,)), ((), ())), preferred_element_type=jnp.float32).astype(dtype)


def activation(gate, up, back, weights):
    sigma = jax.nn.sigmoid(gate)
    scaled = weights * (gate * sigma) * up
    weighted = weights * back
    gate_bar = weighted * up * sigma * (1.0 + gate * (1.0 - sigma))
    up_bar = weighted * gate * sigma
    return scaled.astype(jnp.bfloat16), gate_bar.astype(jnp.bfloat16), up_bar.astype(jnp.bfloat16)


def local(features, expert_rows, route_weight, gate_proj, up_proj, down_proj, out_grad):
    loops = lax.axis_size("loop")
    toks = lax.axis_size("tok")
    me = lax.axis_index("loop")
    tok = lax.axis_index("tok")
    experts, rows = expert_rows.shape
    held, width = features.shape
    panel = gate_proj.shape[2]
    share = rows // toks

    owner = expert_rows // held
    holder = jnp.arange(loops)
    starts = jnp.sum((owner[:, None, :] < holder[None, :, None]).astype(jnp.int32), axis=2)
    start_of = jnp.sum(jnp.where(owner[:, :, None] == holder, starts[:, None, :], 0), axis=2)
    slot = jnp.arange(rows)[None, :] - start_of
    place = owner * SLOTS + slot

    own = jnp.arange(held) + me * held
    hits = expert_rows[:, :, None] == own
    present = jnp.any(hits, axis=1)
    before = jnp.arange(held)[:, None] > jnp.arange(held)[None, :]
    rank = jnp.sum(jnp.where(before[None], present[:, None, :], False).astype(jnp.int32), axis=2)
    pick = (present[:, None, :] & (rank[:, None, :] == jnp.arange(SLOTS)[None, :, None])).astype(jnp.bfloat16)
    pick = pick.reshape(experts * SLOTS, held)
    both = jnp.concatenate([features, out_grad], axis=1)
    sent = dot(pick, both, 1, 0, jnp.bfloat16)

    everyone = lax.all_gather(sent, "loop", axis=0, tiled=False)
    everyone = everyone.reshape(loops, experts, SLOTS, 2 * width)
    spread = (place[:, :, None] == jnp.arange(loops * SLOTS)).astype(jnp.bfloat16)
    compact = [
        dot(spread[e], everyone[:, e].reshape(loops * SLOTS, 2 * width), 1, 0, jnp.bfloat16)
        for e in range(experts)
    ]
    token_rows = [c[:, :width] for c in compact]
    grad_rows = [c[:, width:] for c in compact]

    parts = []
    for e in range(experts):
        parts.append(
            jnp.stack(
                [
                    dot(token_rows[e], gate_proj[e], 1, 0),
                    dot(token_rows[e], up_proj[e], 1, 0),
                    dot(grad_rows[e], down_proj[e], 1, 1),
                ]
            )
        )
    hidden = jnp.stack(parts).reshape(experts, 3, toks, share, panel).transpose(2, 0, 1, 3, 4)
    hidden = lax.all_to_all(hidden.astype(jnp.bfloat16), "tok", 0, 0, tiled=True)
    hidden = jnp.sum(hidden.astype(jnp.float32), axis=0)
    weights = lax.dynamic_slice_in_dim(route_weight, tok * share, share, axis=1)[:, :, None]
    acts = activation(hidden[:, 0], hidden[:, 1], hidden[:, 2], weights)
    acts = lax.all_gather(jnp.stack(acts), "tok", axis=0, tiled=False)
    acts = acts.transpose(1, 2, 0, 3, 4).reshape(3, experts, rows, panel)
    scaled, gate_bar, up_bar = acts[0], acts[1], acts[2]

    out_part = jnp.concatenate([dot(scaled[e], down_proj[e], 1, 0) for e in range(experts)], axis=0)
    in_part = jnp.concatenate(
        [dot(gate_bar[e], gate_proj[e], 1, 1) + dot(up_bar[e], up_proj[e], 1, 1) for e in range(experts)],
        axis=0,
    )
    summed = lax.psum_scatter(
        jnp.concatenate([out_part, in_part], axis=1), "loop", scatter_dimension=0, tiled=True
    ).astype(jnp.bfloat16)
    summed = lax.all_gather(summed, "loop", axis=0, tiled=True)
    home = (expert_rows.reshape(-1)[None, :] == own[:, None]).astype(jnp.bfloat16)
    result = dot(home, summed, 1, 0, jnp.bfloat16)
    mixed, feature_grad = result[:, :width], result[:, width:]

    gate_grad = jnp.stack([dot(token_rows[e], gate_bar[e], 0, 0, jnp.bfloat16) for e in range(experts)])
    up_grad = jnp.stack([dot(token_rows[e], up_bar[e], 0, 0, jnp.bfloat16) for e in range(experts)])
    down_grad = jnp.stack([dot(scaled[e], grad_rows[e], 0, 0, jnp.bfloat16) for e in range(experts)])
    return (mixed, feature_grad, gate_grad, up_grad, down_grad)


def solution(mesh):
    placed = (
        P("loop", "tok"),
        P(),
        P(),
        P(None, "tok", "loop"),
        P(None, "tok", "loop"),
        P(None, "loop", "tok"),
        P("loop", "tok"),
    )
    return jax.shard_map(
        local,
        mesh=mesh,
        in_specs=placed,
        out_specs=(
            P("loop", "tok"),
            P("loop", "tok"),
            P(None, "tok", "loop"),
            P(None, "tok", "loop"),
            P(None, "loop", "tok"),
        ),
        check_vma=False,
    )
```

time: 798 us -> 460 us (0.58)
  waiting for transfers between devices: 703 us -> 388 us
  other arithmetic: 37.1 us -> 17 us
    psum x1 -> x0, waiting for transfers between devices: 341 us -> none  [local(): gate_full, up_full = lax.psum((gate_part, up_part), 'tok')]
    reduce_scatter x2 -> x1, waiting for transfers between devices: 234 us -> 124 us  [local(): lax.psum_scatter(jnp.concatenate([out_part, in_part], axis=1), 'loop', sc...]
    all_gather x2 -> x3, waiting for transfers between devices: 127 us -> 208 us  [the longest x1 76.8 us: local(): acts = lax.all_gather(jnp.stack(acts), 'tok', axis=0, tiled=False)]
    all_to_all x0 -> x1, waiting for transfers between devices: none -> 55.8 us  [local(): lax.all_to_all(hidden.astype(jnp.bfloat16), 'tok', 0, 0, tiled=True)]
    scatter-add x2 -> x0, other arithmetic: 27.9 us -> none  [the longest x1 14 us: local(): out_buffer = jnp.zeros((total_tokens, width), jnp.float32).at[flat_rows]....]
    gather x2 -> x0, local copies, waits for them, and re-layouts: 15.8 us -> none  [the longest x1 8.23 us: local(): grad_rows = grad_everyone[expert_rows]]
    dot_general x9 -> x22, matrix products: 23.7 us -> 21.2 us  [dot(): lax.dot_general(a, b, (((ca,), (cb,)), ((), ())), preferred_element_type=...]
  transfers between devices with their start and end apart: 5 -> 5, of which waited for: 5 -> 5; matrix products, arithmetic and copies ran while one was open for 5% -> 2% of each run, Pallas kernels for 0% -> 0%
where the time goes in v1:
time: 460 us
  waiting for transfers between devices  388 us (84%)
  matrix products  21.2 us (5%)
  other arithmetic  17 us (4%)
  between operations  14.2 us (3%)
  local copies, waits for them, and re-layouts  12.7 us (3%)
  starting transfers between devices  6.57 us (1%)
    reduce_scatter x1, waiting for transfers between devices, local(): lax.psum_scatter(jnp.concatenate([out_part, in_part], axis=1), 'loop', sc...  124 us
    all_gather x1, waiting for transfers between devices, local(): acts = lax.all_gather(jnp.stack(acts), 'tok', axis=0, tiled=False)  76.8 us
    all_gather x1, waiting for transfers between devices, local(): everyone = lax.all_gather(sent, 'loop', axis=0, tiled=False)  70.2 us
    all_gather x1, waiting for transfers between devices, local(): summed = lax.all_gather(summed, 'loop', axis=0, tiled=True)  61.2 us
    all_to_all x1, waiting for transfers between devices, local(): lax.all_to_all(hidden.astype(jnp.bfloat16), 'tok', 0, 0, tiled=True)  55.8 us
    dot_general x22, matrix products, dot(): lax.dot_general(a, b, (((ca,), (cb,)), ((), ())), preferred_element_type=...  21.2 us
  transfers between devices with their start and end apart: 5, of which 5 were waited for; matrix products, arithmetic and copies ran while one was open for 2% of the time, Pallas kernels for 0%

profile of v1, /device:TPU:1, one launch (start us, length us, event | category | flops | bytes accessed | tf_op | source)
XLA Modules:
  0.0 459.5 jit_solution(10095555304861489586)
XLA Ops:
  7.2 0.0 all-gather.8.cloned.1.call-start
  7.3 0.1 eq.90
  7.4 1.0 compare_reduce_fusion
  8.3 0.1 convert_reduce_fusion.2
  8.5 0.1 fusion.51
  8.6 1.8 convolution_convert_fusion.13
  10.4 0.0 all-gather.8.cloned.1.call-update
  10.4 0.7 and_select_fusion
  11.1 0.1 convert_reduce_fusion.1
  11.3 0.1 select_reduce_fusion
  11.4 0.7 subtract_add_fusion
  12.1 1.5 iota_compare_fusion
  13.6 70.2 %all-gather.8.cloned.1.call-done = bf16[3072,1024]{1,0:T(8,128)(2,1)} async-done(((bf16[96,1024]{1,0:T(8,128)(2,1)}), bf16[3072,1024]{1,0:T(8,128)(2,1)}) %all-gather.8.cloned.1.call-update) | async-done | bytes 6291472 | tf_op jit(solution)/shard_map/all_gather | solution.py:49
  83.8 3.7 fusion.59
  87.5 2.6 fusion.2
  90.2 0.1 fusion.61
  90.3 1.6 copy-done.12
  91.9 0.6 fusion.4
  92.5 0.6 fusion.5
  93.1 2.6 fusion.3
  95.8 0.1 fusion.62
  95.9 0.6 fusion.7
  96.5 0.4 copy-done.8
  96.9 0.6 fusion.8
  97.5 0.6 fusion.6
  98.1 0.6 fusion.9
  98.7 0.9 maximum_bitcast_fusion
  99.6 2.5 copy.16
  102.1 6.2 %all-to-all-start = ((bf16[8,2,3,96,448]{4,3,2,1,0:T(8,128)(2,1)}), bf16[8,2,3,96,448]{4,3,2,1,0:T(8,128)(2,1)}, u32[]{:S(2)}, u32[]{:S(2)}) async-start(bf16[8,2,3,96,448]{4,3,2,1,0:T(8,128)(2,1)} %copy.16), calls=%async_computation | async-start | bytes 9437184 | tf_op jit(solution)/shard_map/all_to_all | solution.py:71
  108.4 0.2 all-gather.10.cloned.1.call-start
  108.6 0.1 constant_dynamic-slice_fusion
  108.7 55.8 %all-to-all-done = bf16[8,2,3,96,448]{4,3,2,1,0:T(8,128)(2,1)} async-done(((bf16[8,2,3,96,448]{4,3,2,1,0:T(8,128)(2,1)}), bf16[8,2,3,96,448]{4,3,2,1,0:T(8,128)(2,1)}, u32[]{:S(2)}, u32[]{:S(2)}) %all-to-all-start) | async-done | bytes 4128800 | tf_op jit(solution)/shard_map/all_to_all | solution.py:71
  164.5 3.3 convert_reduce_fusion
  167.8 0.3 multiply_convert_fusion.2
  168.1 0.9 pad_maximum_fusion.3
  169.0 0.0 all-gather.10.cloned.1.call-update
  169.0 0.0 reduce-scatter.2.cloned.1.call-start
  169.1 76.8 %all-gather.10.cloned.1.call-done = bf16[24,2,96,448]{3,2,1,0:T(8,128)(2,1)} async-done(((bf16[3,2,96,448]{3,2,1,0:T(8,128)(2,1)}), bf16[24,2,96,448]{3,2,1,0:T(8,128)(2,1)}) %all-gather.10.cloned.1.call-update) | async-done | bytes 4128784 | tf_op jit(solution)/shard_map/all_gather | solution.py:75
  245.9 2.7 fusion.60
  248.7 0.6 fusion.31
  249.2 0.6 fusion.23
  249.8 0.6 copy-done.15
  250.4 0.6 fusion.18
  251.0 0.6 fusion.26
  251.5 0.0 copy-done.11
  251.6 0.6 convolution_add_fusion.1
  252.2 0.6 convolution_add_fusion
  252.7 3.3 maximum_maximum_fusion
  256.1 0.0 reduce-scatter.2.cloned.1.call-update
  256.1 0.0 all-gather.6.cloned.1.call-start
  256.1 123.6 %reduce-scatter.2.cloned.1.call-done = f32[48,1024]{1,0:T(8,128)} async-done(((f32[1536,1024]{1,0:T(8,128)}), f32[48,1024]{1,0:T(8,128)}) %reduce-scatter.2.cloned.1.call-update) | async-done | bytes 196624 | tf_op jit(solution)/shard_map/reduce_scatter | solution.py:84
  379.8 1.6 convert_element_type.89
  381.4 0.0 all-gather.6.cloned.1.call-update
  381.4 1.8 fusion.14
  383.3 0.5 fusion.15
  383.8 1.0 pad_maximum_fusion.2
  384.8 0.6 fusion.10
  385.4 0.6 fusion.12
  386.0 0.6 fusion.11
  386.6 0.6 fusion.13
  387.2 1.4 pad_maximum_fusion
  388.6 61.2 %all-gather.6.cloned.1.call-done = bf16[1536,1024]{1,0:T(8,128)(2,1)} async-done(((bf16[48,1024]{1,0:T(8,128)(2,1)}), bf16[1536,1024]{1,0:T(8,128)(2,1)}) %all-gather.6.cloned.1.call-update) | async-done | bytes 3145744 | tf_op jit(solution)/shard_map/all_gather | solution.py:87
  449.7 2.5 convolution_convert_fusion.12
  452.2 0.7 fusion.63
  (34 shorter events, 0.1 us)
Async XLA Ops:
  7.2 101.4 %copy-start = (f32[2,768]{1,0:T(2,128)S(1)}, f32[2,768]{1,0:T(2,128)}, u32[]{:S(2)}) copy-start(f32[2,768]{1,0:T(2,128)} %param.9) | copy-start | bytes 18436
  7.2 76.7 %all-gather.8.cloned.1.call-start = ((), (), s32[]{:S(2)}) async-start(), calls=%async_computation.4 | async-start | bytes 6488064 | tf_op jit(solution)/shard_map/all_gather | solution.py:49
  90.1 2.4 copy-start.6
  90.1 1.8 copy-start.12
  90.2 2.3 copy-start.10
  95.8 1.2 copy-start.8
  95.9 1.6 copy-start.14
  102.1 62.4 %all-to-all-start = ((bf16[8,2,3,96,448]{4,3,2,1,0:T(8,128)(2,1)}), bf16[8,2,3,96,448]{4,3,2,1,0:T(8,128)(2,1)}, u32[]{:S(2)}, u32[]{:S(2)}) async-start(bf16[8,2,3,96,448]{4,3,2,1,0:T(8,128)(2,1)} %copy.16), calls=%async_computation | async-start | bytes 9437184 | tf_op jit(solution)/shard_map/all_to_all | solution.py:71
  108.4 137.5 %all-gather.10.cloned.1.call-start = ((), (), s32[]{:S(2)}) async-start(), calls=%async_computation.5 | async-start | bytes 5308416 | tf_op jit(solution)/shard_map/all_gather | solution.py:75
  169.0 210.8 %reduce-scatter.2.cloned.1.call-start = ((), (), s32[]{:S(2)}) async-start(), calls=%async_computation.2 | async-start | bytes 6488064 | tf_op jit(solution)/shard_map/reduce_scatter | solution.py:84
  245.9 2.8 copy-start.13
  248.6 2.9 copy-start.4
  248.6 3.5 copy-start.2
  248.7 1.7 copy-start.15
  250.4 1.2 copy-start.11
  256.1 125.3 %copy-start.16 = (s32[2,768]{1,0:T(2,128)S(1)}, s32[2,768]{1,0:T(2,128)}, u32[]{:S(2)}) copy-start(s32[2,768]{1,0:T(2,128)} %param.8) | copy-start | bytes 18436
  256.1 193.6 %all-gather.6.cloned.1.call-start = ((), (), s32[]{:S(2)}) async-start(), calls=%async_computation.3 | async-start | bytes 3244032 | tf_op jit(solution)/shard_map/all_gather | solution.py:87
  381.4 1.8 copy-start.9
  383.2 1.6 copy-start.7
  383.8 1.6 copy-start.5
  385.4 1.2 copy-start.3
  387.2 65.8 %copy-start.1 = (f32[2,768]{1,0:T(2,128)S(1)}, f32[2,768]{1,0:T(2,128)}, u32[]{:S(2)}) copy-start(f32[2,768]{1,0:T(2,128)} %param.9) | copy-start | bytes 18436
Sparse Core Ops, SparseCore 0:
  10.5 73.2 all-gather.7
  169.1 76.6 all-gather.9
  256.2 123.5 reduce-scatter.1
  382.1 67.6 all-gather.5

commit v2 on v1

--- a/solution.py
+++ b/solution.py
@@ -1,7 +1,460 @@
+import functools
 import jax
 import jax.numpy as jnp
 from jax import lax
+from jax.experimental import pallas as pl
+from jax.experimental.pallas import tpu as pltpu
+
 from jax.sharding import PartitionSpec as P
+
+MESH = pl.DeviceIdType.MESH
+ANY = pl.BlockSpec(memory_space=pl.ANY)
+VM = pl.BlockSpec(memory_space=pltpu.VMEM)
+
+
+def greet(peers):
+    barrier = pltpu.get_barrier_semaphore()
+    for peer in peers:
+        pl.semaphore_signal(barrier, inc=1, device_id=peer, device_id_type=MESH)
+    pl.semaphore_wait(barrier, len(peers))
+
+
+class Sender:
+    def __init__(self, send_sems, recv_sems):
+        self.send_sems, self.recv_sems, self.copies = send_sems, recv_sems, []
+
+    def start(self, src, dst, peer):
+        k = len(self.copies)
+        copy = pltpu.make_async_remote_copy(
+            src_ref=src, dst_ref=dst, send_sem=self.send_sems.at[k], recv_sem=self.recv_sems.at[k],
+            device_id=peer, device_id_type=MESH)
+        copy.start()
+        self.copies.append(copy)
+        return copy
+
+    def drain(self):
+        for copy in self.copies:
+            copy.wait_send()
+
+
+def loop_place():
+    me = lax.axis_index("loop")
+    core = lax.rem(me, 2)
+    side = lax.rem(me // 2, 2)
+    layer = me // 4
+    return layer, side, core
+
+
+LAYERS = 8
+
+
+def loop_index(layer, side, core):
+    return lax.rem(layer + LAYERS, LAYERS) * 4 + side * 2 + core
+
+
+def gather_loop_kernel(src, dst, send_sems, recv_sems, own_sem):
+    layer, side, core = loop_place()
+    other = 1 - side
+    at = lambda d, s, c: loop_index(layer + d, s, c)
+    up, down = {"loop": at(1, side, core)}, {"loop": at(-1, side, core)}
+    across, twin = {"loop": at(0, other, core)}, {"loop": at(0, side, 1 - core)}
+    greet((up, down, across, twin))
+    own = at(0, side, core)
+    sender = Sender(send_sems, recv_sems)
+    waits = []
+
+    keep = pltpu.make_async_copy(src, dst.at[own], own_sem)
+    keep.start()
+    first = sender.start(src.at[0], dst.at[own, 0], across)
+    run = {}
+    hops = {("own", 1): 3, ("own", -1): 4, ("mate", 1): 4, ("mate", -1): 3, ("q", 1): 4, ("q", -1): 3}
+
+    def step(kind, way, s, ref=None):
+        half = 1 if kind == "q" else 0
+        block = at(-way * (s - 1), other if kind == "mate" else side, core)
+        ref = dst.at[block, half] if ref is None else ref
+        run[kind, way, s] = sender.start(ref, dst.at[block, half], up if way == 1 else down)
+
+    for way in (1, -1):
+        step("q", way, 1, src.at[1])
+        step("own", way, 1, src.at[0])
+    twins = [sender.start(src, dst.at[own], twin)]
+    crossed = [sender.start(src.at[1], dst.at[own, 1], across)]
+    first.wait_recv()
+    for way in (1, -1):
+        step("mate", way, 1)
+    mate = at(0, other, core)
+    twins.append(sender.start(dst.at[mate, 0], dst.at[mate, 0], twin))
+    done = 0
+
+    def relay_crossed(block):
+        crossed[len(relayed)].wait_recv()
+        relayed.append(block)
+        twins.append(sender.start(dst.at[block, 1], dst.at[block, 1], twin))
+
+    relayed = []
+    order = [(0, 0)]
+    for s in range(1, 5):
+        for kind in ("q", "own", "mate"):
+            for way in (1, -1):
+                if s > hops[kind, way]:
+                    continue
+                run[kind, way, s].wait_recv()
+                half = 1 if kind == "q" else 0
+                block = at(-way * s, other if kind == "mate" else side, core)
+                if s < hops[kind, way]:
+                    step(kind, way, s + 1)
+                if kind == "q":
+                    crossed.append(sender.start(dst.at[block, 1], dst.at[block, 1], across))
+                    order.append((way, s))
+                twins.append(sender.start(dst.at[block, half], dst.at[block, half], twin))
+        while len(relayed) < len(order) - 2:
+            way, r = order[len(relayed)]
+            relay_crossed(at(-way * r, other, core))
+    while len(relayed) < len(order):
+        way, r = order[len(relayed)]
+        relay_crossed(at(-way * r, other, core))
+    for copy in twins:
+        copy.wait_recv()
+    sender.drain()
+    keep.wait()
+
+
+N_LOOP = 21 + 1 + 8 + 31 + 1
+
+
+def gather_loop(block, collective_id, space=ANY):
+    return pl.pallas_call(
+        gather_loop_kernel,
+        out_shape=jax.ShapeDtypeStruct((32,) + block.shape, block.dtype),
+        in_specs=[VM],
+        out_specs=space,
+        scratch_shapes=[
+            pltpu.SemaphoreType.DMA((N_LOOP,)),
+            pltpu.SemaphoreType.DMA((N_LOOP,)),
+            pltpu.SemaphoreType.DMA,
+        ],
+        compiler_params=pltpu.CompilerParams(collective_id=collective_id, has_side_effects=True),
+        name=f"gather_loop_{collective_id}",
+    )(block)
+
+
+def reduce_loop_kernel(part, out, total, mail, crossing, landing, send_sems, recv_sems):
+    layer, side, core = loop_place()
+    other = 1 - side
+    up, down = ({"loop": loop_index(layer + d, side, core)} for d in (1, -1))
+    across, twin = {"loop": loop_index(layer, other, core)}, {"loop": loop_index(layer, side, 1 - core)}
+    greet((up, down, across, twin))
+    sender = Sender(send_sems, recv_sems)
+    spot = lambda d: lax.rem(layer + d + LAYERS, LAYERS)
+    far_first = (4, 3, -3, 2, -2, 1, -1, 0)
+
+    twins = {}
+    for d in far_first:
+        twins[d] = sender.start(part.at[spot(d), :, 1 - core], total.at[spot(d)], twin)
+    crossed = {}
+
+    def settle(d):
+        twins[d].wait_recv()
+        total[spot(d)] = total[spot(d)] + part[spot(d), :, core]
+        crossed[d] = sender.start(total.at[spot(d), other, 1], crossing.at[far_first.index(d)], across)
+
+    hops = {("own", 1): 4, ("own", -1): 3, ("mate", 1): 3, ("mate", -1): 4, ("q", 1): 4, ("q", -1): 3}
+    run, ready = {}, set()
+    kinds = ("own", "mate", "q")
+
+    def mine(kind, d):
+        who = other if kind == "mate" else side
+        return total.at[spot(d), who, 1 if kind == "q" else 0]
+
+    def box(kind, way, j):
+        return mail.at[kinds.index(kind), (0 if way == 1 else 1), j - 1]
+
+    def send(kind, way, j):
+        if j > hops[kind, way]:
+            return
+        d = way * j if j < 4 else 4
+        if kind == "q" and d not in ready:
+            ready.add(d)
+            crossed[d].wait_recv()
+            total[spot(d), side, 1] = total[spot(d), side, 1] + crossing[far_first.index(d)]
+        src = mine(kind, d)
+        if j < hops[kind, way]:
+            run[kind, way, j + 1].wait_recv()
+            held = box(kind, way, j + 1)
+            held[...] = held[...] + src[...]
+            src = held
+        run[kind, way, j] = sender.start(src, box(kind, way, j), up if way == 1 else down)
+
+    settle(4)
+    for j in (4, 3, 2, 1):
+        for way in (1, -1):
+            send("own", way, j)
+            send("mate", way, j)
+            if j < 4:
+                send("q", way, j + 1)
+        if j > 1:
+            settle(j - 1)
+            settle(1 - j)
+        else:
+            settle(0)
+    for way in (1, -1):
+        send("q", way, 1)
+
+    def arrived(kind):
+        for way in (1, -1):
+            run[kind, way, 1].wait_recv()
+        return mine(kind, 0)[...] + box(kind, 1, 1)[...] + box(kind, -1, 1)[...]
+
+    landing[0] = arrived("mate")
+    last = sender.start(landing.at[0], landing.at[1], across)
+    crossed[0].wait_recv()
+    total[spot(0), side, 1] = total[spot(0), side, 1] + crossing[far_first.index(0)]
+    own = arrived("own")
+    out[1] = arrived("q")
+    last.wait_recv()
+    out[0] = own + landing[1]
+    sender.drain()
+
+
+N_SUM = 8 + 8 + 21 + 1
+
+
+def reduce_loop(part, collective_id):
+    layers, sides, cores, halves, rows, width = part.shape
+    piece = (halves, rows, width)
+    return pl.pallas_call(
+        reduce_loop_kernel,
+        out_shape=jax.ShapeDtypeStruct(piece, part.dtype),
+        in_specs=[VM],
+        out_specs=VM,
+        scratch_shapes=[
+            pltpu.VMEM((layers, sides) + piece, part.dtype),
+            pltpu.VMEM((3, 2, 4, rows, width), part.dtype),
+            pltpu.VMEM((layers, rows, width), part.dtype),
+            pltpu.VMEM((2, rows, width), part.dtype),
+            pltpu.SemaphoreType.DMA((N_SUM,)),
+            pltpu.SemaphoreType.DMA((N_SUM,)),
+        ],
+        compiler_params=pltpu.CompilerParams(collective_id=collective_id, has_side_effects=True, vmem_limit_bytes=48 << 20),
+        name=f"reduce_loop_{collective_id}",
+    )(part)
+
+
+def tok_place():
+    layer, side, core = loop_place()
+    tok = lax.axis_index("tok")
+    tall, high = tok // 2, lax.rem(tok, 2)
+    step = lambda d: lax.rem(tall + d + 4, 4) * 2 + high
+    peers = {
+        "up": {"tok": step(1)},
+        "down": {"tok": step(-1)},
+        "low": {"loop": loop_index(layer, 1 - side, core)},
+        "cross": {"loop": loop_index(layer, 1 - side, core), "tok": tall * 2 + 1 - high},
+    }
+    return tall, high, peers
+
+
+def gather_tok_body(src, dst, transit, sender, tall, high, peers, keep=None):
+    half_rows = src.shape[1] // 2
+    A, B = pl.ds(0, half_rows), pl.ds(half_rows, half_rows)
+    at = lambda d, h: lax.rem(tall + d + 4, 4) * 2 + h
+    other = 1 - high
+    own, mate = at(0, high), at(0, other)
+    sent = {}
+
+    def hop(ref, n):
+        sent["low", n] = sender.start(ref.at[A], transit.at[n, 0], peers["low"])
+        sent["cross", n] = sender.start(ref.at[B], transit.at[n, 1], peers["cross"])
+
+    def pass_on(n, d, half):
+        sent["low", n].wait_recv()
+        sent["to", n, 0] = sender.start(transit.at[n, 0], dst.at[at(d, high), half, A], peers["cross"])
+        sent["cross", n].wait_recv()
+        sent["to", n, 1] = sender.start(transit.at[n, 1], dst.at[at(d, other), half, B], peers["low"])
+
+    def landed(n):
+        sent["to", n, 0].wait_recv()
+        sent["to", n, 1].wait_recv()
+
+    def ring(kind, ref, h, half):
+        sent[kind, 1] = sender.start(ref, dst.at[at(0, h), half], peers["up"])
+        sent[kind, -1] = sender.start(ref, dst.at[at(0, h), half], peers["down"])
+
+    def onward(kind, h, half):
+        for way, piece, to in ((1, A, "up"), (-1, B, "down")):
+            sent[kind, way].wait_recv()
+            ref = dst.at[at(-way, h), half, piece]
+            sent[kind, way, 2] = sender.start(ref, ref, peers[to])
+
+    def closed(kind):
+        sent[kind, 1, 2].wait_recv()
+        sent[kind, -1, 2].wait_recv()
+
+    hop(src.at[0], 0)
+    ring("q", src.at[1], high, 1)
+    ring("p", src.at[0], high, 0)
+    hop(src.at[1], 1)
+    pass_on(0, 0, 0)
+    onward("q", high, 1)
+    hop(dst.at[at(-1, high), 1], 2)
+    hop(dst.at[at(1, high), 1], 3)
+    landed(0)
+    ring("m", dst.at[mate, 0], other, 0)
+    pass_on(1, 0, 1)
+    onward("p", high, 0)
+    closed("q")
+    hop(dst.at[at(2, high), 1], 4)
+    pass_on(2, -1, 1)
+    pass_on(3, 1, 1)
+    onward("m", other, 0)
+    pass_on(4, 2, 1)
+    closed("p")
+    closed("m")
+    for n in range(1, 5):
+        landed(n)
+
+
+N_GT = 5 * 4 + 3 * 4
+
+
+def gather_tok_kernel(src, dst, transit, send_sems, recv_sems, own_sem):
+    tall, high, peers = tok_place()
+    greet(tuple(peers.values()))
+    keep = pltpu.make_async_copy(src, dst.at[tall * 2 + high], own_sem)
+    keep.start()
+    sender = Sender(send_sems, recv_sems)
+    gather_tok_body(src, dst, transit, sender, tall, high, peers)
+    sender.drain()
+    keep.wait()
+
+
+def gather_tok(block, collective_id, space=ANY):
+    halves, rows, width = block.shape
+    return pl.pallas_call(
+        gather_tok_kernel,
+        out_shape=jax.ShapeDtypeStruct((8,) + block.shape, block.dtype),
+        in_specs=[VM],
+        out_specs=space,
+        scratch_shapes=[
+            pltpu.VMEM((5, 2, rows // 2, width), block.dtype),
+            pltpu.SemaphoreType.DMA((N_GT,)),
+            pltpu.SemaphoreType.DMA((N_GT,)),
+            pltpu.SemaphoreType.DMA,
+        ],
+        compiler_params=pltpu.CompilerParams(collective_id=collective_id, has_side_effects=True),
+        name=f"gather_tok_{collective_id}",
+    )(block)
+
+
+N_RT = 5 * 4 + 3 * 4
+
+
+def reduce_tok_kernel(part, out, post, mail, transit, landing, carry, send_sems, recv_sems):
+    tall, high, peers = tok_place()
+    greet(tuple(peers.values()))
+    sender = Sender(send_sems, recv_sems)
+    rows = part.shape[2]
+    half_rows = rows // 2
+    A, B = pl.ds(0, half_rows), pl.ds(half_rows, half_rows)
+    at = lambda d, h: lax.rem(tall + d + 4, 4) * 2 + h
+    other = 1 - high
+    sent = {}
+    f32, bf16 = jnp.float32, jnp.bfloat16
+
+    def hop(n):
+        sent["low", n] = sender.start(post.at[n, A], transit.at[n, 0], peers["low"])
+        sent["cross", n] = sender.start(post.at[n, B], transit.at[n, 1], peers["cross"])
+
+    def pass_on(n):
+        sent["low", n].wait_recv()
+        sent["to", n, 0] = sender.start(transit.at[n, 0], landing.at[n, A], peers["cross"])
+        sent["cross", n].wait_recv()
+        sent["to", n, 1] = sender.start(transit.at[n, 1], landing.at[n, B], peers["low"])
+
+    def landed(n):
+        sent["to", n, 0].wait_recv()
+        sent["to", n, 1].wait_recv()
+
+    def term(kind, d, rows_of):
+        if kind == 2:
+            return carry[DS.index(d), rows_of]
+        return part[at(d, high if kind == 0 else other), 0, rows_of]
+
+    def far(kind):
+        for w, way, piece, to in ((0, 1, A, "up"), (1, -1, B, "down")):
+            mail[kind, w, 0, piece] = term(kind, 2, piece).astype(bf16)
+            sent[kind, way, 2] = sender.start(mail.at[kind, w, 0, piece], mail.at[kind, w, 1, piece], peers[to])
+
+    def near(kind):
+        for w, way, piece, rest, to in ((0, 1, A, B, "up"), (1, -1, B, A, "down")):
+            mail[kind, w, 2, rest] = term(kind, way, rest).astype(bf16)
+            sent[kind, way, 2].wait_recv()
+            mail[kind, w, 2, piece] = (term(kind, way, piece) + mail[kind, w, 1, piece].astype(f32)).astype(bf16)
+            sent[kind, way, 1] = sender.start(mail.at[kind, w, 2], mail.at[kind, w, 3], peers[to])
+
+    def whole(kind):
+        sent[kind, 1, 1].wait_recv()
+        sent[kind, -1, 1].wait_recv()
+        everything = pl.ds(0, rows)
+        return term(kind, 0, everything) + mail[kind, 0, 3].astype(f32) + mail[kind, 1, 3].astype(f32)
+
+    DS = (2, 1, -1, 0)
+    far(1)
+    for n, d in enumerate(DS[:3]):
+        post[n] = part[at(d, other), 1].astype(bf16)
+        hop(n)
+    far(0)
+    post[3] = part[at(0, other), 1].astype(bf16)
+    hop(3)
+    near(1)
+    pass_on(0)
+    near(0)
+    pass_on(1)
+    pass_on(2)
+
+    def mix(n):
+        landed(n)
+        carry[n] = part[at(DS[n], high), 1] + landing[n].astype(f32)
+
+    mix(0)
+    far(2)
+    pass_on(3)
+    post[4] = whole(1).astype(bf16)
+    hop(4)
+    mix(1)
+    mix(2)
+    near(2)
+    pass_on(4)
+    mix(3)
+    out[1] = whole(2)
+    own = whole(0)
+    landed(4)
+    out[0] = own + landing[4].astype(f32)
+    sender.drain()
+
+
+def reduce_tok(part, collective_id):
+    toks, halves, rows, width = part.shape
+    bf16 = jnp.bfloat16
+    return pl.pallas_call(
+        reduce_tok_kernel,
+        out_shape=jax.ShapeDtypeStruct((halves, rows, width), part.dtype),
+        in_specs=[VM],
+        out_specs=VM,
+        scratch_shapes=[
+            pltpu.VMEM((5, rows, width), bf16),
+            pltpu.VMEM((3, 2, 4, rows, width), bf16),
+            pltpu.VMEM((5, 2, rows // 2, width), bf16),
+            pltpu.VMEM((5, rows, width), bf16),
+            pltpu.VMEM((4, rows, width), jnp.float32),
+            pltpu.SemaphoreType.DMA((N_RT,)),
+            pltpu.SemaphoreType.DMA((N_RT,)),
+        ],
+        compiler_params=pltpu.CompilerParams(collective_id=collective_id, has_side_effects=True, vmem_limit_bytes=56 << 20),
+        name=f"reduce_tok_{collective_id}",
+    )(part)
+
 
 SLOTS = 48
 
@@ -46,8 +499,7 @@
     both = jnp.concatenate([features, out_grad], axis=1)
     sent = dot(pick, both, 1, 0, jnp.bfloat16)
 
-    everyone = lax.all_gather(sent, "loop", axis=0, tiled=False)
-    everyone = everyone.reshape(loops, experts, SLOTS, 2 * width)
+    everyone = gather_loop(sent.reshape(experts, SLOTS, 2 * width), 0)
     spread = (place[:, :, None] == jnp.arange(loops * SLOTS)).astype(jnp.bfloat16)
     compact = [
         dot(spread[e], everyone[:, e].reshape(loops * SLOTS, 2 * width), 1, 0, jnp.bfloat16)
@@ -58,36 +510,35 @@
 
     parts = []
     for e in range(experts):
-        parts.append(
-            jnp.stack(
-                [
-                    dot(token_rows[e], gate_proj[e], 1, 0),
-                    dot(token_rows[e], up_proj[e], 1, 0),
-                    dot(grad_rows[e], down_proj[e], 1, 1),
-                ]
-            )
-        )
-    hidden = jnp.stack(parts).reshape(experts, 3, toks, share, panel).transpose(2, 0, 1, 3, 4)
-    hidden = lax.all_to_all(hidden.astype(jnp.bfloat16), "tok", 0, 0, tiled=True)
-    hidden = jnp.sum(hidden.astype(jnp.float32), axis=0)
+        three = [
+            dot(token_rows[e], gate_proj[e], 1, 0),
+            dot(token_rows[e], up_proj[e], 1, 0),
+            dot(grad_rows[e], down_proj[e], 1, 1),
+        ]
+        parts.append(jnp.stack([p.reshape(toks, share, panel) for p in three], axis=1))
+    hidden = jnp.stack(parts, axis=1).reshape(toks, experts, 3 * share, panel)
+    hidden = reduce_tok(hidden, 1).reshape(experts, 3, share, panel)
     weights = lax.dynamic_slice_in_dim(route_weight, tok * share, share, axis=1)[:, :, None]
     acts = activation(hidden[:, 0], hidden[:, 1], hidden[:, 2], weights)
-    acts = lax.all_gather(jnp.stack(acts), "tok", axis=0, tiled=False)
-    acts = acts.transpose(1, 2, 0, 3, 4).reshape(3, experts, rows, panel)
-    scaled, gate_bar, up_bar = acts[0], acts[1], acts[2]
+    acts = jnp.stack(acts, axis=1).reshape(experts, 3 * share, panel)
+    acts = gather_tok(acts, 2).reshape(toks, experts, 3, share, panel)
+    scaled, gate_bar, up_bar = (
+        [acts[:, e, k].reshape(rows, panel) for e in range(experts)] for k in range(3)
+    )
 
     out_part = jnp.concatenate([dot(scaled[e], down_proj[e], 1, 0) for e in range(experts)], axis=0)
     in_part = jnp.concatenate(
         [dot(gate_bar[e], gate_proj[e], 1, 1) + dot(up_bar[e], up_proj[e], 1, 1) for e in range(experts)],
         axis=0,
     )
-    summed = lax.psum_scatter(
-        jnp.concatenate([out_part, in_part], axis=1), "loop", scatter_dimension=0, tiled=True
-    ).astype(jnp.bfloat16)
-    summed = lax.all_gather(summed, "loop", axis=0, tiled=True)
+    shape = (LAYERS, 2, 1, 2, experts * rows // loops, width)
+    part = jnp.concatenate([out_part.reshape(shape), in_part.reshape(shape)], axis=2)
+    summed = reduce_loop(part, 3).astype(jnp.bfloat16)
+    summed = gather_loop(summed, 4).reshape(loops // 2, 2, 2, -1, width)
     home = (expert_rows.reshape(-1)[None, :] == own[:, None]).astype(jnp.bfloat16)
-    result = dot(home, summed, 1, 0, jnp.bfloat16)
-    mixed, feature_grad = result[:, :width], result[:, width:]
+    mixed, feature_grad = (
+        dot(home, summed[:, k].reshape(experts * rows, width), 1, 0, jnp.bfloat16) for k in range(2)
+    )
 
     gate_grad = jnp.stack([dot(token_rows[e], gate_bar[e], 0, 0, jnp.bfloat16) for e in range(experts)])
     up_grad = jnp.stack([dot(token_rows[e], up_bar[e], 0, 0, jnp.bfloat16) for e in range(experts)])

time: 460 us -> 235 us (0.51)
  waiting for transfers between devices: 388 us -> 0 us
  Pallas kernels: 0 us -> 180 us
  between operations: 14.2 us -> 1.01 us
  starting transfers between devices: 6.57 us -> 0 us
    all_gather x3 -> x0, waiting for transfers between devices: 208 us -> none  [the longest x1 76.8 us: local(): acts = lax.all_gather(jnp.stack(acts), 'tok', axis=0, tiled=False)]
    pallas_call x0 -> x5, Pallas kernels: none -> 180 us  [the longest x2 64.2 us: gather_loop(): pl.pallas_call(gather_loop_kernel, out_shape=jax.ShapeDtypeStruct((32,) +...]
    reduce_scatter x1 -> x0, waiting for transfers between devices: 124 us -> none  [local(): lax.psum_scatter(jnp.concatenate([out_part, in_part], axis=1), 'loop', sc...]
    all_to_all x1 -> x0, waiting for transfers between devices: 55.8 us -> none  [local(): lax.all_to_all(hidden.astype(jnp.bfloat16), 'tok', 0, 0, tiled=True)]
    another operation x1 -> x4, other arithmetic: 0.89 us -> 7.18 us  [the longest x1 4.74 us: local(): hidden = jnp.stack(parts, axis=1).reshape(toks, experts, 3 * share, panel)]
    all_to_all x1 -> x0, starting transfers between devices: 6.23 us -> none  [local(): lax.all_to_all(hidden.astype(jnp.bfloat16), 'tok', 0, 0, tiled=True)]
    dot_general x22 -> x23, matrix products: 21.2 us -> 19.6 us  [dot(): lax.dot_general(a, b, (((ca,), (cb,)), ((), ())), preferred_element_type=...]
  transfers between devices with their start and end apart: 5 -> 0, of which waited for: 5 -> 0; matrix products, arithmetic and copies ran while one was open for 2% -> 0% of each run, Pallas kernels for 0% -> 0%
where the time goes in v2:
time: 235 us; the launch traced here: 234 us
  Pallas kernels  180 us (77%)
  matrix products  19.6 us (8%)
  other arithmetic  18.8 us (8%)
  local copies, waits for them, and re-layouts  14.1 us (6%)
    pallas_call x2, Pallas kernels, gather_loop(): pl.pallas_call(gather_loop_kernel, out_shape=jax.ShapeDtypeStruct((32,) +...  64.2 us
    pallas_call x1, Pallas kernels, reduce_tok(): pl.pallas_call(reduce_tok_kernel, out_shape=jax.ShapeDtypeStruct((halves,...  43.5 us
    pallas_call x1, Pallas kernels, reduce_loop(): pl.pallas_call(reduce_loop_kernel, out_shape=jax.ShapeDtypeStruct(piece,...  37.5 us
    pallas_call x1, Pallas kernels, gather_tok(): pl.pallas_call(gather_tok_kernel, out_shape=jax.ShapeDtypeStruct((8,) + b...  35.4 us
    dot_general x23, matrix products, dot(): lax.dot_general(a, b, (((ca,), (cb,)), ((), ())), preferred_element_type=...  19.6 us
    another operation x1, other arithmetic, local(): hidden = jnp.stack(parts, axis=1).reshape(toks, experts, 3 * share, panel)  4.74 us

profile of v2, /device:TPU:1, one launch (start us, length us, event | category | flops | bytes accessed | tf_op | source)
XLA Modules:
  0.0 234.0 jit_solution(12910732234362505927)
XLA Ops:
  0.6 0.0 copy-start
  0.7 1.0 compare_reduce_fusion
  1.7 0.1 convert_reduce_fusion.1
  1.8 0.1 eq.90
  1.9 0.1 fusion.47
  2.0 1.8 convolution_convert_fusion.6
  3.8 38.7 %gather_loop_0.1 = bf16[32,2,48,1024]{3,2,1,0:T(8,128)(2,1)} custom-call(bf16[2,48,1024]{2,1,0:T(8,128)(2,1)} %bitcast.152), custom_call_target="tpu_custom_call" | custom-call | tf_op jit(solution)/shard_map/gather_loop_0/pallas_call | solution.py:127
  42.5 0.0 copy-start.8
  42.5 3.7 %fusion.55 = (bf16[32,1,48,1024]{3,2,1,0:T(8,128)(2,1)S(1)}, bf16[32,1,48,1024]{3,2,1,0:T(8,128)(2,1)S(1)}) fusion(bf16[32,2,48,1024]{3,2,1,0:T(8,128)(2,1)} %gather_loop_0.1), kind=kLoop, calls=%fused_computation.105 | loop fusion | bytes 12582912 | tf_op jit(solution)/shard_map/slice | solution.py:505
  46.2 0.1 convert_reduce_fusion
  46.3 0.1 select_reduce_fusion
  46.5 1.7 iota_compare_fusion
  48.1 2.6 %fusion.2 = bf16[768,1024]{1,0:T(8,128)(2,1)S(1)} fusion(bf16[1536,1024]{1,0:T(8,128)(2,1)S(1)} %bitcast.144, pred[2,768,1536]{2,1,0:T(32,128)(4,1)S(1)} %iota_compare_fusion), kind=kOutput, calls=%fused_computation.11 | convolution fusion | flops 2416705536 | bytes 5898240 | tf_op jit(solution)/shard_map/dot_general | solution.py:463
  50.8 0.0 copy-start.1
  50.8 0.1 fusion.58
  50.9 1.0 copy-done.4
  51.9 0.6 copy-done.1
  52.5 0.6 convolution_bitcast_fusion.4
  53.1 0.0 copy-done.3
  53.2 0.6 convolution_bitcast_fusion.5
  53.8 0.6 copy-done.2
  54.4 0.6 convolution_bitcast_fusion.3
  55.0 0.8 pad_maximum_fusion.2
  55.7 0.5 copy.14
  56.2 2.6 %fusion.3 = bf16[768,1024]{1,0:T(8,128)(2,1)S(1)} fusion(bf16[1536,1024]{1,0:T(8,128)(2,1)S(1)} %bitcast.143, pred[2,768,1536]{2,1,0:T(32,128)(4,1)S(1)} %iota_compare_fusion), kind=kOutput, calls=%fused_computation.12 | convolution fusion | flops 2416705536 | bytes 5898240 | tf_op jit(solution)/shard_map/dot_general | solution.py:463
  58.9 0.1 fusion.59
  59.0 1.0 copy-done.6
  60.1 0.6 convolution_bitcast_fusion.1
  60.6 0.6 convolution_bitcast_fusion.2
  61.2 0.6 convolution_bitcast_fusion
  61.8 0.8 pad_maximum_fusion.3
  62.6 0.5 copy.15
  63.1 4.7 %pad_maximum_fusion.part = f32[8,2,288,448]{3,2,1,0:T(8,128)} fusion(f32[8,1,288,448]{3,2,1,0:T(8,128)S(1)} %bitcast.124, f32[8,1,288,448]{3,2,1,0:T(8,128)S(1)} %bitcast.123), kind=kLoop, calls=%fused_computation | loop fusion | flops 2064384 | bytes 16515072 | tf_op jit(solution)/shard_map/stack | solution.py:519
  67.9 43.5 %reduce_tok_1.1 = f32[2,288,448]{2,1,0:T(8,128)} custom-call(f32[8,2,288,448]{3,2,1,0:T(8,128)} %pad_maximum_fusion.part), custom_call_target="tpu_custom_call" | custom-call | tf_op jit(solution)/shard_map/reduce_tok_1/pallas_call | solution.py:440
  111.3 0.1 constant_dynamic-slice_fusion
  111.4 1.5 multiply_convert_fusion.2
  112.9 0.9 pad_maximum_fusion.9
  113.8 35.4 %gather_tok_2.1 = bf16[8,2,288,448]{3,2,1,0:T(8,128)(2,1)} custom-call(bf16[2,288,448]{2,1,0:T(8,128)(2,1)} %bitcast.151), custom_call_target="tpu_custom_call" | custom-call | tf_op jit(solution)/shard_map/gather_tok_2/pallas_call | solution.py:334
  149.2 2.7 %fusion.56 = (bf16[8,1,1,96,448]{4,3,2,1,0:T(8,128)(2,1)S(1)}, bf16[8,1,1,96,448]{4,3,2,1,0:T(8,128)(2,1)S(1)}, bf16[8,1,1,96,448]{4,3,2,1,0:T(8,128)(2,1)S(1)},...) fusion(bf16[8,2,3,96,448]{4,3,2,1,0:T(8,128)(2,1)} %bitcast.122), kind=kLoop, calls=%fused_computation.106 | loop fusion | bytes 8257536 | tf_op jit(solution)/shard_map/slice | solution.py:526
  152.0 0.1 copy-done.5
  152.0 0.5 fusion.8
  152.6 0.8 copy-done.7
  153.4 0.6 fusion.9
  153.9 1.0 pad_maximum_fusion.8
  154.9 0.6 fusion.4
  155.5 0.6 fusion.6
  156.1 0.6 fusion.5
  156.7 0.6 fusion.7
  157.3 1.4 pad_maximum_fusion.6
  158.6 0.6 fusion.13
  159.2 0.6 fusion.21
  159.8 0.3 pad_maximum_fusion.4
  160.1 0.6 fusion.26
  160.7 0.6 convolution_add_fusion.1
  161.2 0.6 fusion.18
  161.8 0.6 convolution_add_fusion
  162.4 0.3 pad_maximum_fusion.5
  162.7 3.4 %pad_maximum_fusion.1.part = f32[8,2,2,2,48,512]{5,4,3,2,1,0:T(8,128)} fusion(f32[8,2,1,2,48,512]{5,4,3,2,1,0:T(8,128)S(1)} %bitcast.127, f32[8,2,1,2,48,512]{5,4,3,2,1,0:T(8,128)S(1)} %bitcast.126), kind=kLoop, calls=%fused_computation.2 | loop fusion | flops 1572864 | bytes 12582912 | tf_op jit(solution)/shard_map/concatenate | solution.py:535
  166.1 37.5 %reduce_loop_3.1 = f32[2,48,512]{2,1,0:T(8,128)S(1)} custom-call(f32[8,2,2,2,48,512]{5,4,3,2,1,0:T(8,128)} %pad_maximum_fusion.1.part), custom_call_target="tpu_custom_call" | custom-call | tf_op jit(solution)/shard_map/reduce_loop_3/pallas_call | solution.py:226
  203.6 0.7 convert_element_type.65.src
  204.2 25.5 %gather_loop_4.1 = bf16[32,2,48,512]{3,2,1,0:T(8,128)(2,1)} custom-call(bf16[2,48,512]{2,1,0:T(8,128)(2,1)} %convert_element_type.65.src), custom_call_target="tpu_custom_call" | custom-call | tf_op jit(solution)/shard_map/gather_loop_4/pallas_call | solution.py:127
  229.8 2.1 fusion.57
  231.9 1.1 convolution_convert_fusion.7
  233.0 1.1 convolution_convert_fusion.8
  (14 shorter events, 0.1 us)
Async XLA Ops:
  0.6 110.7 %copy-start = (f32[2,768]{1,0:T(2,128)S(1)}, f32[2,768]{1,0:T(2,128)}, u32[]{:S(2)}) copy-start(f32[2,768]{1,0:T(2,128)} %param.9) | copy-start | bytes 18436
  42.5 3.7 %copy-start.8 = (s32[2,768]{1,0:T(2,128)S(1)}, s32[2,768]{1,0:T(2,128)}, u32[]{:S(2)}) copy-start(s32[2,768]{1,0:T(2,128)} %param.8) | copy-start | bytes 18436
  50.8 1.1 copy-start.4
  50.8 1.8 copy-start.1
  51.9 1.2 copy-start.3
  53.2 1.2 copy-start.2
  58.9 1.2 copy-start.6
  149.2 2.8 %copy-start.5 = (bf16[768,1024]{1,0:T(8,128)(2,1)S(1)}, bf16[768,1024]{1,0:T(8,128)(2,1)}, u32[]{:S(2)}) copy-start(bf16[768,1024]{1,0:T(8,128)(2,1)} %copy-done.4) | copy-start | bytes 4718596
  151.9 1.4 copy-start.7

commit v3 on v2

v3 whole, which is shorter than its diff:
```python
import jax
import jax.numpy as jnp
from jax import lax
from jax.experimental import pallas as pl
from jax.experimental.pallas import tpu as pltpu

from jax.sharding import PartitionSpec as P

MESH = pl.DeviceIdType.MESH
ANY = pl.BlockSpec(memory_space=pl.ANY)
VM = pl.BlockSpec(memory_space=pltpu.VMEM)


def greet(peers):
    barrier = pltpu.get_barrier_semaphore()
    for peer in peers:
        pl.semaphore_signal(barrier, inc=1, device_id=peer, device_id_type=MESH)
    pl.semaphore_wait(barrier, len(peers))


class Sender:
    def __init__(self, send_sems, recv_sems):
        self.send_sems, self.recv_sems, self.copies = send_sems, recv_sems, []

    def start(self, src, dst, peer):
        k = len(self.copies)
        copy = pltpu.make_async_remote_copy(
            src_ref=src, dst_ref=dst, send_sem=self.send_sems.at[k], recv_sem=self.recv_sems.at[k],
            device_id=peer, device_id_type=MESH)
        copy.start()
        self.copies.append(copy)
        return copy

    def drain(self):
        for copy in self.copies:
            copy.wait_send()


def loop_place():
    me = lax.axis_index("loop")
    core = lax.rem(me, 2)
    side = lax.rem(me // 2, 2)
    layer = me // 4
    return layer, side, core


LAYERS = 8


def loop_index(layer, side, core):
    return lax.rem(layer + LAYERS, LAYERS) * 4 + side * 2 + core


def loop_peers(layer, side, core):
    return {
        "up": {"loop": loop_index(layer + 1, side, core)},
        "down": {"loop": loop_index(layer - 1, side, core)},
        "across": {"loop": loop_index(layer, 1 - side, core)},
        "twin": {"loop": loop_index(layer, side, 1 - core)},
    }


RUNS = {("own", 1): 3, ("own", -1): 4, ("mate", 1): 4, ("mate", -1): 3, ("q", 1): 4, ("q", -1): 3}


def gather_loop_body(src, dst, sender):
    layer, side, core = loop_place()
    other = 1 - side
    at = lambda d, s, c: loop_index(layer + d, s, c)
    peers = loop_peers(layer, side, core)
    own, mate = at(0, side, core), at(0, other, core)
    run, twins, crossed, order = {}, [], [], [(0, 0)]

    def step(kind, way, s, ref=None):
        half = 1 if kind == "q" else 0
        block = at(-way * (s - 1), other if kind == "mate" else side, core)
        ref = dst.at[half, block] if ref is None else ref
        run[kind, way, s] = sender.start(ref, dst.at[half, block], peers["up" if way == 1 else "down"])

    def double(half, block, ref=None):
        ref = dst.at[half, block] if ref is None else ref
        twins.append(sender.start(ref, dst.at[half, block], peers["twin"]))

    def relay():
        n = len(relayed)
        way, r = order[n]
        crossed[n].wait_recv()
        relayed.append(n)
        double(1, at(-way * r, other, core))

    relayed = []
    first = sender.start(src.at[0], dst.at[0, own], peers["across"])
    for way in (1, -1):
        step("q", way, 1, src.at[1])
        step("own", way, 1, src.at[0])
    for half in (0, 1):
        double(half, own, src.at[half])
    crossed.append(sender.start(src.at[1], dst.at[1, own], peers["across"]))
    first.wait_recv()
    for way in (1, -1):
        step("mate", way, 1)
    double(0, mate)
    for s in range(1, 5):
        for kind in ("q", "own", "mate"):
            for way in (1, -1):
                if s > RUNS[kind, way]:
                    continue
                run[kind, way, s].wait_recv()
                half = 1 if kind == "q" else 0
                block = at(-way * s, other if kind == "mate" else side, core)
                if s < RUNS[kind, way]:
                    step(kind, way, s + 1)
                if kind == "q":
                    crossed.append(sender.start(dst.at[1, block], dst.at[1, block], peers["across"]))
                    order.append((way, s))
                double(half, block)
        while len(relayed) < len(order) - 2:
            relay()
    while len(relayed) < len(order):
        relay()
    for copy in twins:
        copy.wait_recv()


N_LOOP = 21 + 1 + 8 + 32


def gather_loop_kernel(src, dst, send_sems, recv_sems, own_sems):
    place = loop_place()
    greet(tuple(loop_peers(*place).values()))
    own = loop_index(*place)
    keep = [pltpu.make_async_copy(src.at[h], dst.at[h, own], own_sems.at[h]) for h in (0, 1)]
    for copy in keep:
        copy.start()
    sender = Sender(send_sems, recv_sems)
    gather_loop_body(src, dst, sender)
    sender.drain()
    for copy in keep:
        copy.wait()


def gather_loop(block, collective_id, space=ANY):
    halves, rows, width = block.shape
    return pl.pallas_call(
        gather_loop_kernel,
        out_shape=jax.ShapeDtypeStruct((halves, 32, rows, width), block.dtype),
        in_specs=[VM],
        out_specs=space,
        scratch_shapes=[
            pltpu.SemaphoreType.DMA((N_LOOP,)),
            pltpu.SemaphoreType.DMA((N_LOOP,)),
            pltpu.SemaphoreType.DMA((2,)),
        ],
        compiler_params=pltpu.CompilerParams(collective_id=collective_id, has_side_effects=True),
        name=f"gather_loop_{collective_id}",
    )(block)


HOPS = {("own", 1): 4, ("own", -1): 3, ("mate", 1): 3, ("mate", -1): 4, ("q", 1): 4, ("q", -1): 3}
FAR_FIRST = (4, 3, -3, 2, -2, 1, -1, 0)


def reduce_loop_body(part, make, total, mail, crossing, landing, sender):
    layer, side, core = loop_place()
    other = 1 - side
    peers = loop_peers(layer, side, core)
    spot = lambda d: lax.rem(layer + d + LAYERS, LAYERS)
    twins, crossed, run, ready = {}, {}, {}, set()
    kinds = ("own", "mate", "q")

    def offer(d):
        make(spot(d))
        twins[d] = sender.start(part.at[spot(d), 1 - core], total.at[spot(d)], peers["twin"])

    def settle(d):
        twins[d].wait_recv()
        total[spot(d)] = total[spot(d)] + part[spot(d), core]
        crossed[d] = sender.start(total.at[spot(d), other, 1], crossing.at[FAR_FIRST.index(d)], peers["across"])

    def mine(kind, d):
        who = other if kind == "mate" else side
        return total.at[spot(d), who, 1 if kind == "q" else 0]

    def box(kind, way, j):
        return mail.at[kinds.index(kind), (0 if way == 1 else 1), j - 1]

    def blend(d):
        if d not in ready:
            ready.add(d)
            crossed[d].wait_recv()
            total[spot(d), side, 1] = total[spot(d), side, 1] + crossing[FAR_FIRST.index(d)]

    def send(kind, way, j):
        if j > HOPS[kind, way]:
            return
        d = way * j if j < 4 else 4
        if kind == "q":
            blend(d)
        src = mine(kind, d)
        if j < HOPS[kind, way]:
            run[kind, way, j + 1].wait_recv()
            held = box(kind, way, j + 1)
            held[...] = held[...] + src[...]
            src = held
        run[kind, way, j] = sender.start(src, box(kind, way, j), peers["up" if way == 1 else "down"])

    offer(4)
    offer(3)
    offer(-3)
    settle(4)
    for j in (4, 3, 2, 1):
        for way in (1, -1):
            send("own", way, j)
            send("mate", way, j)
            if j < 4:
                send("q", way, j + 1)
        if j > 2:
            offer(j - 2)
            offer(2 - j)
        elif j == 2:
            offer(0)
        if j > 1:
            settle(j - 1)
            settle(1 - j)
        else:
            settle(0)
    for way in (1, -1):
        send("q", way, 1)

    def arrived(kind):
        for way in (1, -1):
            run[kind, way, 1].wait_recv()
        return mine(kind, 0)[...] + box(kind, 1, 1)[...] + box(kind, -1, 1)[...]

    landing[0] = arrived("mate")
    last = sender.start(landing.at[0], landing.at[1], peers["across"])
    blend(0)
    own = arrived("own")
    q = arrived("q")
    last.wait_recv()
    return own + landing[1], q


N_SUM = 8 + 8 + 21 + 1


def finish_kernel(acts, gate_w, up_w, down_w, tokens, out, part, total, mail, crossing, landing, piece, everyone,
                  send_sems, recv_sems, send2, recv2, own_sems):
    layer, side, core = loop_place()
    greet(tuple(loop_peers(layer, side, core).values()))
    share = acts.shape[2] // 3
    bf16 = jnp.bfloat16

    def make(z):
        e, y = z // 4, lax.rem(z, 4)
        scaled, gate_bar, up_bar = (
            jnp.concatenate([acts[2 * y + h, e, pl.ds(k * share, share)] for h in (0, 1)], axis=0) for k in range(3)
        )
        mixed = mm(scaled, down_w[e], 1, 0)
        back = mm(gate_bar, gate_w[e], 1, 1) + mm(up_bar, up_w[e], 1, 1)
        part[z, 0] = mixed.reshape(part.shape[2:])
        part[z, 1] = back.reshape(part.shape[2:])

    sender = Sender(send_sems, recv_sems)
    p, q = reduce_loop_body(part, make, total, mail, crossing, landing, sender)
    piece[0] = p.astype(bf16)
    piece[1] = q.astype(bf16)
    own = loop_index(layer, side, core)
    keep = [pltpu.make_async_copy(piece.at[h], everyone.at[h, own], own_sems.at[h]) for h in (0, 1)]
    for copy in keep:
        copy.start()
    later = Sender(send2, recv2)
    gather_loop_body(piece, everyone, later)
    for copy in keep:
        copy.wait()
    held = out.shape[1]
    lanes = tokens[...]
    mine = lax.broadcasted_iota(jnp.int32, (held, lanes.shape[1]), 0) + own * held
    home = jnp.where(mine == lanes, 1.0, 0.0).astype(bf16)
    rows, width = everyone.shape[2:]
    for k in range(2):
        rows_k = jnp.concatenate(
            [everyone[h, 2 * n + k] for n in range(16) for h in (0, 1)], axis=0
        )
        out[k] = mm(home, rows_k, 1, 0).astype(bf16)
    sender.drain()
    later.drain()


def mm(a, b, ca, cb):
    return lax.dot_general(a, b, (((ca,), (cb,)), ((), ())), preferred_element_type=jnp.float32)


def finish(acts, gate_w, up_w, down_w, tokens, held, collective_id):
    width = down_w.shape[2]
    rows = tokens.shape[1] // 32
    f32, bf16 = jnp.float32, jnp.bfloat16
    piece = (2, rows, width)
    dma = pltpu.SemaphoreType.DMA
    return pl.pallas_call(
        finish_kernel,
        out_shape=jax.ShapeDtypeStruct((2, held, width), bf16),
        in_specs=[VM] * 5,
        out_specs=VM,
        scratch_shapes=[
            pltpu.VMEM((LAYERS, 2, 2) + piece, f32),
            pltpu.VMEM((LAYERS, 2) + piece, f32),
            pltpu.VMEM((3, 2, 4, rows, width), f32),
            pltpu.VMEM((LAYERS, rows, width), f32),
            pltpu.VMEM((2, rows, width), f32),
            pltpu.VMEM(piece, bf16),
            pltpu.VMEM((2, 32, rows, width), bf16),
            dma((N_SUM,)), dma((N_SUM,)), dma((N_LOOP,)), dma((N_LOOP,)), dma((2,)),
        ],
        compiler_params=pltpu.CompilerParams(collective_id=collective_id, has_side_effects=True, vmem_limit_bytes=56 << 20),
        name="finish",
    )(acts, gate_w, up_w, down_w, tokens)


def tok_place():
    layer, side, core = loop_place()
    tok = lax.axis_index("tok")
    tall, high = tok // 2, lax.rem(tok, 2)
    step = lambda d: lax.rem(tall + d + 4, 4) * 2 + high
    peers = {
        "up": {"tok": step(1)},
        "down": {"tok": step(-1)},
        "low": {"loop": loop_index(layer, 1 - side, core)},
        "cross": {"loop": loop_index(layer, 1 - side, core), "tok": tall * 2 + 1 - high},
    }
    return tall, high, peers


def gather_tok_body(src, dst, transit, sender, tall, high, peers, keep=None):
    half_rows = src.shape[1] // 2
    A, B = pl.ds(0, half_rows), pl.ds(half_rows, half_rows)
    at = lambda d, h: lax.rem(tall + d + 4, 4) * 2 + h
    other = 1 - high
    own, mate = at(0, high), at(0, other)
    sent = {}

    def hop(ref, n):
        sent["low", n] = sender.start(ref.at[A], transit.at[n, 0], peers["low"])
        sent["cross", n] = sender.start(ref.at[B], transit.at[n, 1], peers["cross"])

    def pass_on(n, d, half):
        sent["low", n].wait_recv()
        sent["to", n, 0] = sender.start(transit.at[n, 0], dst.at[at(d, high), half, A], peers["cross"])
        sent["cross", n].wait_recv()
        sent["to", n, 1] = sender.start(transit.at[n, 1], dst.at[at(d, other), half, B], peers["low"])

    def landed(n):
        sent["to", n, 0].wait_recv()
        sent["to", n, 1].wait_recv()

    def ring(kind, ref, h, half):
        sent[kind, 1] = sender.start(ref, dst.at[at(0, h), half], peers["up"])
        sent[kind, -1] = sender.start(ref, dst.at[at(0, h), half], peers["down"])

    def onward(kind, h, half):
        for way, piece, to in ((1, A, "up"), (-1, B, "down")):
            sent[kind, way].wait_recv()
            ref = dst.at[at(-way, h), half, piece]
            sent[kind, way, 2] = sender.start(ref, ref, peers[to])

    def closed(kind):
        sent[kind, 1, 2].wait_recv()
        sent[kind, -1, 2].wait_recv()

    hop(src.at[0], 0)
    ring("q", src.at[1], high, 1)
    ring("p", src.at[0], high, 0)
    hop(src.at[1], 1)
    pass_on(0, 0, 0)
    onward("q", high, 1)
    hop(dst.at[at(-1, high), 1], 2)
    hop(dst.at[at(1, high), 1], 3)
    landed(0)
    ring("m", dst.at[mate, 0], other, 0)
    pass_on(1, 0, 1)
    onward("p", high, 0)
    closed("q")
    hop(dst.at[at(2, high), 1], 4)
    pass_on(2, -1, 1)
    pass_on(3, 1, 1)
    onward("m", other, 0)
    pass_on(4, 2, 1)
    closed("p")
    closed("m")
    for n in range(1, 5):
        landed(n)


def reduce_tok_body(part, make, settled, post, mail, transit, landing, carry, sender, tall, high, peers):
    rows = part.shape[2]
    half_rows = rows // 2
    A, B = pl.ds(0, half_rows), pl.ds(half_rows, half_rows)
    at = lambda d, h: lax.rem(tall + d + 4, 4) * 2 + h
    other = 1 - high
    sent = {}
    f32, bf16 = jnp.float32, jnp.bfloat16

    def hop(n):
        sent["low", n] = sender.start(post.at[n, A], transit.at[n, 0], peers["low"])
        sent["cross", n] = sender.start(post.at[n, B], transit.at[n, 1], peers["cross"])

    def pass_on(n):
        sent["low", n].wait_recv()
        sent["to", n, 0] = sender.start(transit.at[n, 0], landing.at[n, A], peers["cross"])
        sent["cross", n].wait_recv()
        sent["to", n, 1] = sender.start(transit.at[n, 1], landing.at[n, B], peers["low"])

    def landed(n):
        sent["to", n, 0].wait_recv()
        sent["to", n, 1].wait_recv()

    def term(kind, d, rows_of):
        if kind == 2:
            return carry[DS.index(d), rows_of]
        return part[at(d, high if kind == 0 else other), 0, rows_of]

    def far(kind):
        for w, way, piece, to in ((0, 1, A, "up"), (1, -1, B, "down")):
            mail[kind, w, 0, piece] = term(kind, 2, piece).astype(bf16)
            sent[kind, way, 2] = sender.start(mail.at[kind, w, 0, piece], mail.at[kind, w, 1, piece], peers[to])

    def near(kind):
        for w, way, piece, rest, to in ((0, 1, A, B, "up"), (1, -1, B, A, "down")):
            mail[kind, w, 2, rest] = term(kind, way, rest).astype(bf16)
            sent[kind, way, 2].wait_recv()
            mail[kind, w, 2, piece] = (term(kind, way, piece) + mail[kind, w, 1, piece].astype(f32)).astype(bf16)
            sent[kind, way, 1] = sender.start(mail.at[kind, w, 2], mail.at[kind, w, 3], peers[to])

    def whole(kind):
        sent[kind, 1, 1].wait_recv()
        sent[kind, -1, 1].wait_recv()
        everything = pl.ds(0, rows)
        return term(kind, 0, everything) + mail[kind, 0, 3].astype(f32) + mail[kind, 1, 3].astype(f32)

    DS = (2, 1, -1, 0)
    make(0, 2)
    far(1)
    far(0)
    for n, d in enumerate(DS[:3]):
        make(1, d)
        post[n] = part[at(d, other), 1].astype(bf16)
        hop(n)
    make(0, 1)
    make(0, -1)
    near(1)
    pass_on(0)
    near(0)
    make(1, 0)
    post[3] = part[at(0, other), 1].astype(bf16)
    hop(3)
    pass_on(1)
    make(0, 0)
    pass_on(2)

    def mix(n):
        landed(n)
        carry[n] = part[at(DS[n], high), 1] + landing[n].astype(f32)

    mix(0)
    far(2)
    pass_on(3)
    post[4] = whole(1).astype(bf16)
    hop(4)
    mix(1)
    mix(2)
    near(2)
    pass_on(4)
    mix(3)
    own = whole(0)
    landed(4)
    settled(0, own + landing[4].astype(f32))
    settled(1, whole(2))


N_T = 5 * 4 + 3 * 4


def hidden_kernel(everyone, place, weight, gate_w, up_w, down_w, acts, rows_out, part, post, mail, transit, landing, carry,
                  turn, transit2, send_sems, recv_sems, send2, recv2, own_sem):
    tall, high, peers = tok_place()
    greet(tuple(peers.values()))
    bf16 = jnp.bfloat16
    width = gate_w.shape[1]
    share = part.shape[2] // 3
    pair = 2 * share
    slots = everyone.shape[1]

    def make(e, d):
        y = lax.rem(tall + d + 4, 4)
        start = pl.multiple_of(y * pair, pair)
        spread = place[e, pl.ds(start, pair)] == lax.broadcasted_iota(jnp.int32, (pair, slots), 1)
        rows = mm(jnp.where(spread, 1.0, 0.0).astype(bf16), everyone[e], 1, 0).astype(bf16)
        rows_out[e, pl.ds(start, pair)] = rows
        gate = mm(rows[:, :width], gate_w[e], 1, 0)
        up = mm(rows[:, :width], up_w[e], 1, 0)
        back = mm(rows[:, width:], down_w[e], 1, 1)
        for h in (0, 1):
            for k, value in enumerate((gate, up, back)):
                part[2 * y + h, e, pl.ds(k * share, share)] = value[h * share : (h + 1) * share]

    def settled(e, sums):
        gate, up, back = (sums[k * share : (k + 1) * share] for k in range(3))
        w = weight[e, pl.ds(pl.multiple_of((tall * 2 + high) * share, share), share)]
        sigma = jax.nn.sigmoid(gate)
        weighted = w * back
        turn[e, pl.ds(0, share)] = (w * (gate * sigma) * up).astype(bf16)
        turn[e, pl.ds(share, share)] = (weighted * up * sigma * (1.0 + gate * (1.0 - sigma))).astype(bf16)
        turn[e, pl.ds(2 * share, share)] = (weighted * gate * sigma).astype(bf16)

    sender = Sender(send_sems, recv_sems)
    reduce_tok_body(part, make, settled, post, mail, transit, landing, carry, sender, tall, high, peers)
    keep = pltpu.make_async_copy(turn, acts.at[tall * 2 + high], own_sem)
    keep.start()
    later = Sender(send2, recv2)
    gather_tok_body(turn, acts, transit2, later, tall, high, peers)
    sender.drain()
    later.drain()
    keep.wait()


def hidden(everyone, place, weight, gate_w, up_w, down_w, toks, collective_id):
    experts, width, panel = gate_w.shape
    total = place.shape[1]
    rows = 3 * total // toks
    f32, bf16 = jnp.float32, jnp.bfloat16
    dma = pltpu.SemaphoreType.DMA
    return pl.pallas_call(
        hidden_kernel,
        out_shape=(
            jax.ShapeDtypeStruct((toks, experts, rows, panel), bf16),
            jax.ShapeDtypeStruct((experts, total, 2 * width), bf16),
        ),
        in_specs=[VM] * 6,
        out_specs=(ANY, VM),
        scratch_shapes=[
            pltpu.VMEM((toks, experts, rows, panel), f32),
            pltpu.VMEM((5, rows, panel), bf16),
            pltpu.VMEM((3, 2, 4, rows, panel), bf16),
            pltpu.VMEM((5, 2, rows // 2, panel), bf16),
            pltpu.VMEM((5, rows, panel), bf16),
            pltpu.VMEM((4, rows, panel), f32),
            pltpu.VMEM((experts, rows, panel), bf16),
            pltpu.VMEM((5, 2, rows // 2, panel), bf16),
            dma((N_T,)), dma((N_T,)), dma((N_T,)), dma((N_T,)), dma,
        ],
        compiler_params=pltpu.CompilerParams(collective_id=collective_id, has_side_effects=True, vmem_limit_bytes=60 << 20),
        name="hidden",
    )(everyone, place, weight, gate_w, up_w, down_w)


SLOTS = 48


def dot(a, b, ca, cb, dtype=jnp.float32):
    return lax.dot_general(a, b, (((ca,), (cb,)), ((), ())), preferred_element_type=jnp.float32).astype(dtype)


def local(features, expert_rows, route_weight, gate_proj, up_proj, down_proj, out_grad):
    loops = lax.axis_size("loop")
    toks = lax.axis_size("tok")
    me = lax.axis_index("loop")
    experts, rows = expert_rows.shape
    held, width = features.shape
    panel = gate_proj.shape[2]
    share = rows // toks

    owner = expert_rows // held
    holder = jnp.arange(loops)
    starts = jnp.sum((owner[:, None, :] < holder[None, :, None]).astype(jnp.int32), axis=2)
    start_of = jnp.sum(jnp.where(owner[:, :, None] == holder, starts[:, None, :], 0), axis=2)
    slot = jnp.arange(rows)[None, :] - start_of
    place = owner * SLOTS + slot

    own = jnp.arange(held) + me * held
    hits = expert_rows[:, :, None] == own
    present = jnp.any(hits, axis=1)
    before = jnp.arange(held)[:, None] > jnp.arange(held)[None, :]
    rank = jnp.sum(jnp.where(before[None], present[:, None, :], False).astype(jnp.int32), axis=2)
    pick = (present[:, None, :] & (rank[:, None, :] == jnp.arange(SLOTS)[None, :, None])).astype(jnp.bfloat16)
    pick = pick.reshape(experts * SLOTS, held)
    both = jnp.concatenate([features, out_grad], axis=1)
    sent = dot(pick, both, 1, 0, jnp.bfloat16)

    everyone = gather_loop(sent.reshape(experts, SLOTS, 2 * width), 0)
    everyone = everyone.reshape(experts, loops * SLOTS, 2 * width)
    acts, compact = hidden(
        everyone, place[:, :, None], route_weight[:, :, None], gate_proj, up_proj, down_proj, toks, 1
    )
    result = finish(acts, gate_proj, up_proj, down_proj, expert_rows.reshape(1, -1), held, 2)
    mixed, feature_grad = result[0], result[1]

    acts = acts.reshape(toks, experts, 3, share, panel)
    scaled, gate_bar, up_bar = (
        [acts[:, e, k].reshape(rows, panel) for e in range(experts)] for k in range(3)
    )
    token_rows = [compact[e, :, :width] for e in range(experts)]
    grad_rows = [compact[e, :, width:] for e in range(experts)]
    gate_grad = jnp.stack([dot(token_rows[e], gate_bar[e], 0, 0, jnp.bfloat16) for e in range(experts)])
    up_grad = jnp.stack([dot(token_rows[e], up_bar[e], 0, 0, jnp.bfloat16) for e in range(experts)])
    down_grad = jnp.stack([dot(scaled[e], grad_rows[e], 0, 0, jnp.bfloat16) for e in range(experts)])
    return (mixed, feature_grad, gate_grad, up_grad, down_grad)


def solution(mesh):
    placed = (
        P("loop", "tok"),
        P(),
        P(),
        P(None, "tok", "loop"),
        P(None, "tok", "loop"),
        P(None, "loop", "tok"),
        P("loop", "tok"),
    )
    return jax.shard_map(
        local,
        mesh=mesh,
        in_specs=placed,
        out_specs=(
            P("loop", "tok"),
            P("loop", "tok"),
            P(None, "tok", "loop"),
            P(None, "tok", "loop"),
            P(None, "loop", "tok"),
        ),
        check_vma=False,
    )
```

time: 235 us -> 202 us (0.86)
  other arithmetic: 18.8 us -> 4.09 us
  matrix products: 19.6 us -> 5.22 us
  local copies, waits for them, and re-layouts: 14.1 us -> 10.7 us
    dot_general x23 -> x7, matrix products: 19.6 us -> 5.22 us  [dot(): lax.dot_general(a, b, (((ca,), (cb,)), ((), ())), preferred_element_type=...]
    another operation x4 -> x0, other arithmetic: 7.18 us -> none  [the longest x1 4.74 us: local(): hidden = jnp.stack(parts, axis=1).reshape(toks, experts, 3 * share, panel)]
    slice x4 -> x0, local copies, waits for them, and re-layouts: 5.99 us -> none  [the longest x1 3.66 us: local(): everyone[:, e].reshape(loops * SLOTS, 2 * width)]
    concatenate x3 -> x0, other arithmetic: 3.98 us -> none  [the longest x1 3.36 us: local(): jnp.concatenate([out_part.reshape(shape), in_part.reshape(shape)], axis=2)]
    broadcast_in_dim x0 -> x2, local copies, waits for them, and re-layouts: none -> 2.37 us  [the longest x1 1.18 us: local(): place[:, :, None]]
    pallas_call x5 -> x3, Pallas kernels: 180 us -> 181 us  [the longest x1 79.8 us: hidden(): pl.pallas_call(hidden_kernel, out_shape=(jax.ShapeDtypeStruct((toks, expe...]
where the time goes in v3:
time: 202 us
  Pallas kernels  181 us (90%)
  local copies, waits for them, and re-layouts  10.7 us (5%)
  matrix products  5.22 us (3%)
  other arithmetic  4.09 us (2%)
    pallas_call x1, Pallas kernels, hidden(): pl.pallas_call(hidden_kernel, out_shape=(jax.ShapeDtypeStruct((toks, expe...  79.8 us
    pallas_call x1, Pallas kernels, finish(): pl.pallas_call(finish_kernel, out_shape=jax.ShapeDtypeStruct((2, held, wi...  62.2 us
    pallas_call x1, Pallas kernels, gather_loop(): pl.pallas_call(gather_loop_kernel, out_shape=jax.ShapeDtypeStruct((halves...  38.8 us
    dot_general x7, matrix products, dot(): lax.dot_general(a, b, (((ca,), (cb,)), ((), ())), preferred_element_type=...  5.22 us

profile of v3, /device:TPU:1, one launch (start us, length us, event | category | flops | bytes accessed | tf_op | source)
XLA Modules:
  0.0 201.5 jit_solution(16404923064970088151)
XLA Ops:
  0.6 1.0 compare_reduce_fusion
  1.6 0.1 convert_reduce_fusion.1
  1.8 0.1 eq.52
  1.9 0.1 fusion.21
  1.9 1.8 convolution_convert_fusion.6
  3.8 0.0 copy-start.2
  3.8 0.0 copy-start
  3.8 0.0 copy-start.1
  3.8 38.8 %gather_loop_0.1 = bf16[2,32,48,1024]{3,2,1,0:T(8,128)(2,1)} custom-call(bf16[2,48,1024]{2,1,0:T(8,128)(2,1)} %bitcast.62), custom_call_target="tpu_custom_call" | custom-call | tf_op jit(solution)/shard_map/gather_loop_0/pallas_call | solution.py:144
  42.6 0.0 copy-start.3
  42.6 0.0 copy-done.2
  42.7 0.1 convert_reduce_fusion
  42.8 0.1 select_reduce_fusion
  42.9 1.2 copy.22.place
  44.1 0.0 copy-done
  44.1 1.3 copy.24.gate_w
  45.4 0.0 copy-done.1
  45.4 1.3 copy.25.up_w
  46.7 0.0 copy-done.3
  46.7 1.2 copy.23.weight
  47.9 79.8 %hidden.1 = (bf16[8,2,288,448]{3,2,1,0:T(8,128)(2,1)}, bf16[2,768,1024]{2,1,0:T(8,128)(2,1)}) custom-call(bf16[2,1536,1024]{2,1,0:T(8,128)(2,1)} %bitcast.60, s32[2,768,1]{2,1,0:T(8,128)} %copy.22.place, f32[2,768,1]{2,1,0:T(8,128)} %copy.23.weight, bf16[2,512,448]{2,1,0:T(8,128)(2,1)} %copy.24.gate_w, bf16[2,512,448]{2,1,0:T(8,128)(2,1)} %copy.25.up_w, ...), custom_call_target="tpu_custom_call" | custom-call | tf_op jit(solution)/shard_map/hidden/pallas_call | solution.py:532
  127.7 0.0 copy-start.4
  127.7 2.8 %fusion.23 = (bf16[8,1,1,96,448]{4,3,2,1,0:T(8,128)(2,1)S(1)}, bf16[8,1,1,96,448]{4,3,2,1,0:T(8,128)(2,1)S(1)}, bf16[8,1,1,96,448]{4,3,2,1,0:T(8,128)(2,1)S(1)},...) fusion(bf16[8,2,3,96,448]{4,3,2,1,0:T(8,128)(2,1)} %bitcast.61), kind=kLoop, calls=%fused_computation.49 | loop fusion | bytes 8257536 | tf_op jit(solution)/shard_map/slice | solution.py:599
  130.5 0.5 copy-done.4
  131.0 0.6 fusion.2
  131.6 0.6 fusion.3
  132.2 0.6 fusion
  132.8 0.6 fusion.1
  133.3 1.6 pad_maximum_fusion
  134.9 0.5 fusion.4
  135.5 0.5 fusion.5
  136.0 1.0 pad_maximum_fusion.2
  137.1 0.6 copy.28
  137.7 62.2 %finish.1 = bf16[2,128,512]{2,1,0:T(8,128)(2,1)} custom-call(bf16[8,2,288,448]{3,2,1,0:T(8,128)(2,1)} %get-tuple-element.7.acts, bf16[2,512,448]{2,1,0:T(8,128)(2,1)} %copy.24.gate_w, bf16[2,512,448]{2,1,0:T(8,128)(2,1)} %copy.25.up_w, bf16[2,448,512]{2,1,0:T(8,128)(2,1)} %down_w.3, s32[1,1536]{1,0:T(1,128)} %bitcast.70), custom_call_target="tpu_custom_call" | custom-call | tf_op jit(solution)/shard_map/finish/pallas_call | solution.py:300
  199.8 1.7 slice_bitcast_fusion
  (5 shorter events, 0.1 us)
Async XLA Ops:
  3.8 38.8 %copy-start.2 = (s32[2,768]{1,0:T(2,128)S(1)}, s32[2,768]{1,0:T(2,128)}, u32[]{:S(2)}) copy-start(s32[2,768]{1,0:T(2,128)} %param.8) | copy-start | bytes 18436
  3.8 40.3 %copy-start = (bf16[2,512,448]{1,2,0:T(8,128)(2,1)S(1)}, bf16[2,512,448]{1,2,0:T(8,128)(2,1)}, u32[]{:S(2)}) copy-start(bf16[2,512,448]{1,2,0:T(8,128)(2,1)} %param.10) | copy-start | bytes 2752516
  3.8 41.6 %copy-start.1 = (bf16[2,512,448]{1,2,0:T(8,128)(2,1)S(1)}, bf16[2,512,448]{1,2,0:T(8,128)(2,1)}, u32[]{:S(2)}) copy-start(bf16[2,512,448]{1,2,0:T(8,128)(2,1)} %param.11) | copy-start | bytes 2752516
  42.6 4.1 %copy-start.3 = (f32[2,768]{1,0:T(2,128)S(1)}, f32[2,768]{1,0:T(2,128)}, u32[]{:S(2)}) copy-start(f32[2,768]{1,0:T(2,128)} %param.9) | copy-start | bytes 18436
  127.7 3.3 %copy-start.4 = (bf16[2,768,1024]{2,1,0:T(8,128)(2,1)S(1)}, bf16[2,768,1024]{2,1,0:T(8,128)(2,1)}, u32[]{:S(2)}) copy-start(bf16[2,768,1024]{2,1,0:T(8,128)(2,1)} %get-tuple-element.8) | copy-start | bytes 9437188

commit v4 on v1

v4 whole, which is shorter than its diff:
```python
import heapq

import jax
import jax.numpy as jnp
from jax import lax
from jax.experimental import pallas as pl
from jax.experimental.pallas import tpu as pltpu
from jax.sharding import PartitionSpec as P

MESH = pl.DeviceIdType.MESH
ANY = pl.BlockSpec(memory_space=pl.ANY)
VM = pl.BlockSpec(memory_space=pltpu.VMEM)
SLOTS = 48
LAYERS = 8
FAR_FIRST = (4, 3, -3, 2, -2, 1, -1, 0)
COPIES = 320
RING = 64


class Sender:
    def __init__(self, send_sems, recv_sems):
        self.send_sems, self.recv_sems, self.copies, self.left = send_sems, recv_sems, [], 0
        self.used, self.spare = 0, []

    def slot(self):
        if self.spare:
            return self.spare.pop(0)
        self.used += 1
        return self.used - 1

    def start(self, src, dst, peer, slot=None):
        k = len(self.copies)
        if k >= RING:
            self.gone(k - RING)
        copy = pltpu.make_async_remote_copy(
            src_ref=src, dst_ref=dst, send_sem=self.send_sems.at[k % RING],
            recv_sem=self.recv_sems.at[self.slot() if slot is None else slot],
            device_id=peer, device_id_type=MESH)
        copy.start()
        copy.number = k
        self.copies.append(copy)
        return copy

    def gone(self, upto):
        while self.left <= upto:
            self.copies[self.left].wait_send()
            self.left += 1

    def all_landed(self, ref, slot, peer):
        pltpu.make_async_remote_copy(
            src_ref=ref, dst_ref=ref, send_sem=self.send_sems.at[0], recv_sem=self.recv_sems.at[slot],
            device_id=peer, device_id_type=MESH).wait_recv()

    def drain(self):
        self.gone(len(self.copies) - 1)


def mm(a, b, ca, cb):
    return lax.dot_general(a, b, (((ca,), (cb,)), ((), ())), preferred_element_type=jnp.float32)


class Agenda:
    def __init__(self):
        self.heap, self.count, self.now = [], 0, 0.0

    def add(self, chain, when):
        heapq.heappush(self.heap, (when, self.count, chain))
        self.count += 1

    def run(self):
        while self.heap:
            when, _, chain = heapq.heappop(self.heap)
            self.now = max(self.now, when)
            due = next(chain, None)
            if due is not None:
                self.add(chain, max(due, when))


def kernel(sent, lanes8, tokens, gate_hbm, up_hbm, down_hbm, out_m, out_f, gate_g, up_g, down_g,
           G, rows_of, part, post, mail, transit, landing, carry, sums, turn, acts, transit2,
           part2, total, box_p, box_q, crossing, joint, piece, everyone, staging, cols, gate_t, up_t, down_w, early,
           send_sems, recv_sems, own_sems, out_sems, in_sems):
    f32, bf16 = jnp.float32, jnp.bfloat16
    me, tok = lax.axis_index("loop"), lax.axis_index("tok")
    core, side, layer = lax.rem(me, 2), lax.rem(me // 2, 2), me // 4
    tall, high = tok // 2, lax.rem(tok, 2)
    far_side, far_high = 1 - side, 1 - high
    spot = lambda d: lax.rem(layer + d + LAYERS, LAYERS)
    at = lambda d, s: spot(d) * 4 + s * 2 + core
    tok_at = lambda d, h: lax.rem(tall + d + 4, 4) * 2 + h
    to = {
        "z+": {"loop": spot(1) * 4 + side * 2 + core},
        "z-": {"loop": spot(-1) * 4 + side * 2 + core},
        "low": {"loop": layer * 4 + far_side * 2 + core},
        "twin": {"loop": layer * 4 + side * 2 + 1 - core},
        "y+": {"tok": tok_at(1, high)},
        "y-": {"tok": tok_at(-1, high)},
        "cross": {"loop": layer * 4 + far_side * 2 + core, "tok": tall * 2 + far_high},
    }
    Z = {1: "z+", -1: "z-"}
    Y = {1: "y+", -1: "y-"}
    loads = [
        pltpu.make_async_copy(src, dst, in_sems.at[n])
        for n, (src, dst) in enumerate(((gate_hbm, gate_t), (up_hbm, up_t), (down_hbm, down_w)))
    ]
    for load in loads:
        load.start()
    barrier = pltpu.get_barrier_semaphore()
    for peer in to.values():
        pl.semaphore_signal(barrier, inc=1, device_id=peer, device_id_type=MESH)
    pl.semaphore_wait(barrier, len(to))

    sender = Sender(send_sems, recv_sems)
    agenda = Agenda()
    own_copies = []

    def keep(src, dst):
        copy = pltpu.make_async_copy(src, dst, own_sems.at[len(own_copies)])
        copy.start()
        own_copies.append(copy)
        return copy

    def spread_loop(src, view, lanes, due, whole):
        run, crossed, order = {}, [], [(0, 0)]
        twin_slot = sender.slot()
        hops = {("own", 1): 3, ("own", -1): 4, ("mate", 1): 4, ("mate", -1): 3, ("q", 1): 4, ("q", -1): 3}
        p = next((n for n, mode in enumerate(lanes) if mode == "P"), None)
        q = next((n for n, mode in enumerate(lanes) if mode == "Q"), None)
        lane = {"own": p, "mate": p, "q": q}
        kinds = [k for k in ("q", "own", "mate") if lane[k] is not None]
        own = at(0, side)

        def step(kind, way, s):
            n = lane[kind]
            block = at(-way * (s - 1), far_side if kind == "mate" else side)
            ref = src(n) if (s == 1 and kind != "mate") else view(n, block)
            run[kind, way, s] = sender.start(ref, view(n, block), to[Z[way]])

        def double(n, block, ref=None):
            sender.start(view(n, block) if ref is None else ref, view(n, block), to["twin"], twin_slot)

        kept = [keep(src(n), view(n, own)) for n in range(len(lanes))]
        if p is not None:
            first = sender.start(src(p), view(p, own), to["low"])
        for kind in kinds:
            if kind != "mate":
                for way in (1, -1):
                    step(kind, way, 1)
        for n in range(len(lanes)):
            double(n, own, src(n))
        if q is not None:
            crossed.append(sender.start(src(q), view(q, own), to["low"]))
        relayed = []

        def relay():
            n = len(relayed)
            way, r = order[n]
            crossed[n].wait_recv()
            relayed.append(n)
            double(q, at(-way * r, far_side))

        yield due[0]
        if p is not None:
            first.wait_recv()
            for way in (1, -1):
                step("mate", way, 1)
            double(p, at(0, far_side))
        for s in range(1, 5):
            yield due[s]
            for kind in kinds:
                for way in (1, -1):
                    if s > hops[kind, way]:
                        continue
                    run[kind, way, s].wait_recv()
                    block = at(-way * s, far_side if kind == "mate" else side)
                    if s < hops[kind, way]:
                        step(kind, way, s + 1)
                    if kind == "q":
                        crossed.append(sender.start(view(q, block), view(q, block), to["low"]))
                        order.append((way, s))
                    double(lane[kind], block)
            while q is not None and len(relayed) < len(order) - 2:
                relay()
        yield due[5]
        while q is not None and len(relayed) < len(order):
            relay()
        yield due[6]
        sender.all_landed(whole, twin_slot, to["twin"])
        for copy in kept:
            copy.wait()

    share = part.shape[2] // 3
    pair = 2 * share
    slots = 32 * SLOTS

    def make(e, d):
        y = lax.rem(tall + d + 4, 4)
        start = pl.multiple_of(y * pair, pair)
        place = cols[pl.ds(start, pair), pl.ds(e, 1)].astype(jnp.int32)
        spread = jnp.where(place == lax.broadcasted_iota(jnp.int32, (pair, slots), 1), 1.0, 0.0).astype(bf16)
        x, dy = (mm(spread, G[e, k].reshape(slots, G.shape[4]), 1, 0).astype(bf16) for k in (0, 1))
        rows_of[e, 0, pl.ds(start, pair)] = x
        rows_of[e, 1, pl.ds(start, pair)] = dy
        for k, value in enumerate((mm(x, gate_t[e], 1, 1), mm(x, up_t[e], 1, 1), mm(dy, down_w[e], 1, 1))):
            for h in (0, 1):
                part[2 * y + h, e, pl.ds(k * share, share)] = value[h * share : (h + 1) * share]

    rows = part.shape[2]
    p_rows = mail.shape[4]
    q_rows = rows - p_rows
    DS = (2, 1, -1, 0)

    class Ferry:
        def __init__(self, passage):
            self.passage, self.sent = passage, {}

        def cut(self, size):
            return pl.ds(0, size // 2), pl.ds(size // 2, size // 2)

        def hop(self, n, ref):
            size = ref.shape[0]
            first, second = self.cut(size)
            half = pl.ds(0, size // 2)
            self.sent[n, 0] = sender.start(ref.at[first], self.passage.at[n, 0, half], to["low"])
            self.sent[n, 1] = sender.start(ref.at[second], self.passage.at[n, 1, half], to["cross"])

        def pass_on(self, n, first_to, second_to, slot=None):
            size = first_to.shape[0]
            first, second = self.cut(size)
            half = pl.ds(0, size // 2)
            self.sent[n, 0].wait_recv()
            self.sent[n, 2] = sender.start(self.passage.at[n, 0, half], first_to.at[first], to["cross"], slot)
            self.sent[n, 1].wait_recv()
            self.sent[n, 3] = sender.start(self.passage.at[n, 1, half], second_to.at[second], to["low"], slot)

        def landed(self, n):
            self.sent[n, 2].wait_recv()
            self.sent[n, 3].wait_recv()

    def settled(e):
        gate, up, back = (sums[e, pl.ds(k * share, share)] for k in range(3))
        w = cols[pl.ds(pl.multiple_of(tok * share, share), share), pl.ds(2 + e, 1)]
        sigma = jax.nn.sigmoid(gate)
        weighted = w * back
        turn[e, pl.ds(0, share)] = (w * (gate * sigma) * up).astype(bf16)
        turn[e, pl.ds(share, share)] = (weighted * up * sigma * (1.0 + gate * (1.0 - sigma))).astype(bf16)
        turn[e, pl.ds(2 * share, share)] = (weighted * gate * sigma).astype(bf16)

    def sum_tok(e, T, f):
        ferry = Ferry(transit.at[e])
        sent_tok = {}
        sizes = {0: p_rows, 1: p_rows, 2: q_rows}
        QR = pl.ds(p_rows, q_rows)

        def term(kind, d, lo, size):
            if kind == 2:
                return carry[e, DS.index(d), pl.ds(lo, size)]
            return part[tok_at(d, high if kind == 0 else far_high), e, pl.ds(lo, size)]

        def ends(kind, w):
            half = sizes[kind] // 2
            return (0, half, half) if w == 0 else (half, 0, half)

        def far(kind):
            for w, way in ((0, 1), (1, -1)):
                lo, _, half = ends(kind, w)
                at_lo = pl.ds(lo, half)
                mail[e, kind, w, 0, at_lo] = term(kind, 2, lo, half).astype(bf16)
                sent_tok[kind, way, 2] = sender.start(
                    mail.at[e, kind, w, 0, at_lo], mail.at[e, kind, w, 1, at_lo], to[Y[way]])

        def near(kind):
            for w, way in ((0, 1), (1, -1)):
                lo, rest, half = ends(kind, w)
                whole_of = pl.ds(0, sizes[kind])
                mail[e, kind, w, 2, pl.ds(rest, half)] = term(kind, way, rest, half).astype(bf16)
                sent_tok[kind, way, 2].wait_recv()
                mail[e, kind, w, 2, pl.ds(lo, half)] = (
                    term(kind, way, lo, half) + mail[e, kind, w, 1, pl.ds(lo, half)].astype(f32)).astype(bf16)
                sent_tok[kind, way, 1] = sender.start(
                    mail.at[e, kind, w, 2, whole_of], mail.at[e, kind, w, 3, whole_of], to[Y[way]])

        def whole(kind):
            sent_tok[kind, 1, 1].wait_recv()
            sent_tok[kind, -1, 1].wait_recv()
            full = pl.ds(0, sizes[kind])
            return (term(kind, 0, 0, sizes[kind]) + mail[e, kind, 0, 3, full].astype(f32)
                    + mail[e, kind, 1, 3, full].astype(f32))

        def give(n):
            make(e, DS[n])
            post[e, n, pl.ds(0, q_rows)] = part[tok_at(DS[n], far_high), e, QR].astype(bf16)
            ferry.hop(n, post.at[e, n, pl.ds(0, q_rows)])

        def pass_on(n):
            spot_of = landing.at[e, n, pl.ds(0, p_rows if n == 4 else q_rows)]
            ferry.pass_on(n, spot_of, spot_of)

        def mix(n):
            ferry.landed(n)
            carry[e, n] = part[tok_at(DS[n], high), e, QR] + landing[e, n, pl.ds(0, q_rows)].astype(f32)

        yield T
        give(0)
        far(1)
        far(0)
        yield T + f * 1.5
        give(1)
        yield T + f * 2.8
        give(2)
        yield T + f * 4.8
        pass_on(0)
        yield T + f * 6.4
        near(1)
        near(0)
        give(3)
        yield T + f * 7.9
        pass_on(1)
        yield T + f * 8.5
        mix(0)
        far(2)
        yield T + f * 10.0
        pass_on(2)
        yield T + f * 12.0
        post[e, 4] = whole(1).astype(bf16)
        ferry.hop(4, post.at[e, 4])
        mix(1)
        yield T + f * 13.0
        pass_on(3)
        yield T + f * 14.0
        mix(2)
        near(2)
        yield T + f * 16.0
        sums[e, pl.ds(0, p_rows)] = whole(0)
        pass_on(4)
        yield T + f * 17.5
        mix(3)
        yield T + f * 19.0
        sums[e, QR] = whole(2)
        yield T + f * 20.0
        ferry.landed(4)
        sums[e, pl.ds(0, p_rows)] = sums[e, pl.ds(0, p_rows)] + landing[e, 4].astype(f32)
        settled(e)

    def spread_tok(e, U, f):
        ferry = Ferry(transit2.at[e])
        sent_back = {}
        part_of = {"p": (0, p_rows), "m": (0, p_rows), "q": (p_rows, q_rows)}
        PR, QR = pl.ds(0, p_rows), pl.ds(p_rows, q_rows)
        side_of = {"p": high, "m": far_high, "q": high}

        def ring(kind, ref):
            lo, size = part_of[kind]
            for way in (1, -1):
                sent_back[kind, way] = sender.start(
                    ref, acts.at[tok_at(0, side_of[kind]), e, pl.ds(lo, size)], to[Y[way]])

        def onward(kind):
            lo, size = part_of[kind]
            for way, start in ((1, lo), (-1, lo + size // 2)):
                sent_back[kind, way].wait_recv()
                ref = acts.at[tok_at(-way, side_of[kind]), e, pl.ds(start, size // 2)]
                sent_back[kind, way, 2] = sender.start(ref, ref, to[Y[way]], None if kind == "q" else ring_slot)

        def closed(kind):
            sent_back[kind, 1, 2].wait_recv()
            sent_back[kind, -1, 2].wait_recv()

        def pass_on(n, d, which):
            ferry.pass_on(n, acts.at[tok_at(d, high), e, which], acts.at[tok_at(d, far_high), e, which],
                          last_slot if n else None)

        last_slot, ring_slot = sender.slot(), sender.slot()
        mine = acts.at[tok_at(0, high), e]
        kept = keep(turn.at[e], mine)
        ferry.hop(0, turn.at[e, PR])
        ring("q", turn.at[e, QR])
        ring("p", turn.at[e, PR])
        ferry.hop(1, turn.at[e, QR])
        yield U + f * 4.0
        pass_on(0, 0, PR)
        yield U + f * 4.6
        onward("q")
        ferry.hop(2, acts.at[tok_at(-1, high), e, QR])
        ferry.hop(3, acts.at[tok_at(1, high), e, QR])
        yield U + f * 6.5
        pass_on(1, 0, QR)
        yield U + f * 7.5
        ferry.landed(0)
        ring("m", acts.at[tok_at(0, far_high), e, PR])
        onward("p")
        yield U + f * 8.5
        closed("q")
        ferry.hop(4, acts.at[tok_at(2, high), e, QR])
        yield U + f * 9.5
        pass_on(2, -1, QR)
        yield U + f * 12.0
        pass_on(3, 1, QR)
        yield U + f * 13.0
        onward("m")
        yield U + f * 14.5
        pass_on(4, 2, QR)
        yield U + f * 16.0
        sender.all_landed(acts.at[pl.ds(0, 2), e, PR], ring_slot, to["y+"])
        yield U + f * 18.0
        sender.all_landed(acts.at[pl.ds(0, 4), e, QR], last_slot, to["cross"])
        kept.wait()

    def product(e, z):
        scaled, gate_bar, up_bar = (acts[z, e, pl.ds(k * share, share)] for k in range(3))
        part2[z, 0] = mm(scaled, down_w[e], 1, 0).reshape(part2.shape[2:])
        part2[z, 1] = (mm(gate_bar, gate_t[e], 1, 0) + mm(up_bar, up_t[e], 1, 0)).reshape(part2.shape[2:])

    last_offers, unsettled = [], set()

    def sum_loop(e, lanes, result, start, due):
        twins, crossed, run, ready = {}, {}, {}, set()
        hops = {("own", 1): 4, ("own", -1): 3, ("mate", 1): 3, ("mate", -1): 4, ("q", 1): 4, ("q", -1): 3}
        p, q = lanes.get("P"), lanes.get("Q")
        kinds = (["own", "mate"] if p else []) + (["q"] if q else [])
        yield start
        while unsettled:
            start += 0.5
            yield start
        for copy in last_offers:
            sender.gone(copy.number)
        last_offers.clear()
        unsettled.update(FAR_FIRST)

        def offer(d):
            product(e, spot(d))
            twins[d] = sender.start(part2.at[spot(d), 1 - core], total.at[e, spot(d)], to["twin"])
            last_offers.append(twins[d])

        def settle(d):
            unsettled.remove(d)
            twins[d].wait_recv()
            total[e, spot(d)] = total[e, spot(d)] + part2[spot(d), core]
            if q:
                crossed[d] = sender.start(
                    total.at[e, spot(d), far_side, q], crossing.at[e, FAR_FIRST.index(d), pl.ds(0, q.size)], to["low"])

        def mine(kind, d):
            return total.at[e, spot(d), far_side if kind == "mate" else side, q if kind == "q" else p]

        def box(kind, way, j):
            w = 0 if way == 1 else 1
            if kind == "q":
                return box_q.at[e, w, j - 1, pl.ds(0, q.size)]
            return box_p.at[e, 0 if kind == "own" else 1, w, j - 1, pl.ds(0, p.size)]

        def blend(d):
            if d not in ready:
                ready.add(d)
                crossed[d].wait_recv()
                total[e, spot(d), side, q] = (
                    total[e, spot(d), side, q] + crossing[e, FAR_FIRST.index(d), pl.ds(0, q.size)])

        def send(kind, way, j):
            if j > hops[kind, way]:
                return
            d = way * j if j < 4 else 4
            if kind == "q":
                blend(d)
            src = mine(kind, d)
            if j < hops[kind, way]:
                run[kind, way, j + 1].wait_recv()
                held = box(kind, way, j + 1)
                held[...] = held[...] + src[...]
                src = held
            run[kind, way, j] = sender.start(src, box(kind, way, j), to[Z[way]])

        for n, d in enumerate((4, 3, -3)):
            offer(d)
            yield start + 0.4 * n
        settle(4)
        for j in (4, 3, 2, 1):
            for kind in kinds:
                for way in (1, -1):
                    if kind != "q":
                        send(kind, way, j)
                    elif j < 4:
                        send(kind, way, j + 1)
            if j > 2:
                offer(j - 2)
                offer(2 - j)
            elif j == 2:
                offer(0)
            yield due[4 - j]
            for d in ((j - 1, 1 - j) if j > 1 else (0,)):
                settle(d)
        if q:
            for way in (1, -1):
                send("q", way, 1)
        yield due[4]

        def arrived(kind):
            for way in (1, -1):
                run[kind, way, 1].wait_recv()
            return mine(kind, 0)[...] + box(kind, 1, 1)[...] + box(kind, -1, 1)[...]

        if p:
            joint[e, 0, pl.ds(0, p.size)] = arrived("mate")
            last = sender.start(joint.at[e, 0, pl.ds(0, p.size)], joint.at[e, 1, pl.ds(0, p.size)], to["low"])
            own = arrived("own")
        if q:
            blend(0)
            piece[result, q] = arrived("q").astype(bf16)
        yield due[5]
        if p:
            last.wait_recv()
            piece[result, p] = (own + joint[e, 1, pl.ds(0, p.size)]).astype(bf16)

    def weight_grads(e):
        acts_of = lambda k: jnp.concatenate([acts[t, e, pl.ds(k * share, share)] for t in range(8)], axis=0)
        for n, (k, arr, dst) in enumerate(((1, 0, gate_g), (2, 0, up_g), (0, 1, down_g))):
            staging[n, e] = mm(acts_of(k), rows_of[e, arr], 0, 0).astype(bf16)
            copy = pltpu.make_async_copy(staging.at[n, e], dst.at[e], out_sems.at[n, e])
            copy.start()
            out_copies.append(copy)
            yield agenda.now + 3.0

    out_copies = []

    def gather_in(e, due):
        return spread_loop(lambda n: sent.at[e, n], lambda n, block: G.at[e, n, block], ("P", "Q"), due, G.at[e, 0])

    def chain(e):
        start = (0.0, 12.0)[e]
        yield from gather_in(e, tuple(start + t for t in ((3, 4, 8, 12, 16, 19, 21), (3, 7, 11, 15, 19.5, 23, 25))[e]))
        if e == 0:
            for load in loads:
                load.wait()
        yield from sum_tok(e, (22.0, 38.0)[e], (1.3, 1.6)[e])
        yield from spread_tok(e, (50.0, 73.0)[e], 1.5)
        agenda.add(weight_grads(e), agenda.now + 3.0)
        S = (80.0, 102.0)[e]
        yield from sum_loop(e, {"P": pl.ds(0, SLOTS // 2), "Q": pl.ds(SLOTS // 2, SLOTS // 2)}, e, S,
                            tuple(S + t for t in (3.5, 8.5, 13.5, 17.5, 20, 23)))
        R = (106.0, 127.0)[e]
        yield from spread_loop(lambda n: piece.at[e], lambda n, block: everyone.at[e, block], ("PQ"[e],),
                               tuple(R + t for t in ((4, 8, 12, 16, 20, 22, 24), (2.5, 4.5, 7, 9.5, 12, 13, 14))[e]),
                               everyone.at[e, pl.ds(0, 16)])
        partial_result(e)

    held = out_m.shape[0]

    def partial_result(e):
        lanes = tokens[pl.ds(e, 1)]
        mine = lax.broadcasted_iota(jnp.int32, (held, lanes.shape[1]), 0) + me * held
        home = jnp.where(mine == lanes, 1.0, 0.0).astype(bf16)
        for k, dst in enumerate((out_m, out_f)):
            found = jnp.concatenate([everyone[e, 2 * n + k] for n in range(16)], axis=0)
            value = mm(home, found, 1, 0)
            if e == 0:
                early[k] = value
            else:
                dst[...] = (early[k] + value).astype(bf16)

    def columns():
        cols[...] = jnp.transpose(jnp.concatenate([lanes8[...], jnp.zeros((120, cols.shape[0]), f32)], axis=0))
        yield

    agenda.add(chain(0), 0.0)
    agenda.add(columns(), 2.0)
    agenda.add(chain(1), 12.0)
    agenda.run()

    sender.drain()
    for copy in out_copies:
        copy.wait()


def everything(sent, lanes8, tokens, gate_t, up_t, down_w, held):
    experts, panel, width = down_w.shape
    total = lanes8.shape[1]
    toks = 8
    rows = 3 * total // toks
    p_rows = 160
    q_rows = rows - p_rows
    f32, bf16 = jnp.float32, jnp.bfloat16
    dma = pltpu.SemaphoreType.DMA
    V = pltpu.VMEM
    grads = jax.ShapeDtypeStruct((experts, panel, width), bf16)
    return pl.pallas_call(
        kernel,
        out_shape=(jax.ShapeDtypeStruct((held, width), bf16),) * 2 + (grads,) * 3,
        in_specs=[VM] * 3 + [ANY] * 3,
        out_specs=(VM, VM, ANY, ANY, ANY),
        scratch_shapes=[
            V((experts, 2, 32, SLOTS, width), bf16),
            V((experts, 2, total, width), bf16),
            V((toks, experts, rows, panel), f32),
            V((experts, 5, p_rows, panel), bf16),
            V((experts, 3, 2, 4, p_rows, panel), bf16),
            V((experts, 5, 2, p_rows // 2, panel), bf16),
            V((experts, 5, p_rows, panel), bf16),
            V((experts, 4, q_rows, panel), f32),
            V((experts, rows, panel), f32),
            V((experts, rows, panel), bf16),
            V((toks, experts, rows, panel), bf16),
            V((experts, 5, 2, p_rows // 2, panel), bf16),
            V((LAYERS, 2, 2, SLOTS, width), f32),
            V((experts, LAYERS, 2, SLOTS, width), f32),
            V((experts, 2, 2, 4, SLOTS // 2, width), f32),
            V((experts, 2, 4, SLOTS // 2, width), f32),
            V((experts, LAYERS, SLOTS // 2, width), f32),
            V((experts, 2, SLOTS // 2, width), f32),
            V((experts, SLOTS, width), bf16),
            V((experts, 32, SLOTS, width), bf16),
            V((3, experts, panel, width), bf16),
            V((total, 128), f32),
            V((experts, panel, width), bf16), V((experts, panel, width), bf16), V((experts, panel, width), bf16),
            V((2, held, width), f32),
            dma((RING,)), dma((COPIES,)), dma((12,)), dma((3, experts)), dma((3,)),
        ],
        compiler_params=pltpu.CompilerParams(
            collective_id=0, has_side_effects=True, vmem_limit_bytes=67_043_328),
        name="everything",
    )(sent, lanes8, tokens, gate_t, up_t, down_w)


def hand_over_kernel(*refs):
    n = len(refs) // 2
    for src, dst in zip(refs[:n], refs[n:]):
        dst[...] = src[...]


def hand_over(*arrays):
    return pl.pallas_call(
        hand_over_kernel,
        out_shape=tuple(jax.ShapeDtypeStruct(a.shape, a.dtype) for a in arrays),
        in_specs=[VM] * len(arrays),
        out_specs=(VM,) * len(arrays),
        name="hand_over",
    )(*arrays)


def local(features, expert_rows, route_weight, gate_proj, up_proj, down_proj, out_grad):
    loops = lax.axis_size("loop")
    me = lax.axis_index("loop")
    experts, rows = expert_rows.shape
    held, width = features.shape

    owner = expert_rows // held
    holder = jnp.arange(loops)
    starts = jnp.sum((owner[:, None, :] < holder[None, :, None]).astype(jnp.int32), axis=2)
    start_of = jnp.sum(jnp.where(owner[:, :, None] == holder, starts[:, None, :], 0), axis=2)
    place = owner * SLOTS + jnp.arange(rows)[None, :] - start_of
    lanes8 = jnp.concatenate([place.astype(jnp.float32), route_weight, jnp.zeros((4, rows), jnp.float32)], axis=0)

    own = jnp.arange(held) + me * held
    present = jnp.any(expert_rows[:, :, None] == own, axis=1)
    before = jnp.arange(held)[:, None] > jnp.arange(held)[None, :]
    rank = jnp.sum(jnp.where(before[None], present[:, None, :], False).astype(jnp.int32), axis=2)
    pick = (present[:, None, :] & (rank[:, None, :] == jnp.arange(SLOTS)[None, :, None])).astype(jnp.bfloat16)
    pick = pick.reshape(experts * SLOTS, held)
    sent = jnp.stack(
        [mm(pick, v, 1, 0).astype(jnp.bfloat16).reshape(experts, SLOTS, width) for v in (features, out_grad)], axis=1
    )
    mixed, feature_grad, gate_grad, up_grad, down_grad = everything(
        sent, lanes8, expert_rows, jnp.swapaxes(gate_proj, 1, 2), jnp.swapaxes(up_proj, 1, 2),
        down_proj, held)
    mixed, feature_grad, gate_grad, up_grad, down_grad = hand_over(mixed, feature_grad, gate_grad, up_grad, down_grad)
    return (mixed, feature_grad, jnp.swapaxes(gate_grad, 1, 2), jnp.swapaxes(up_grad, 1, 2), down_grad)


def solution(mesh):
    placed = (
        P("loop", "tok"),
        P(),
        P(),
        P(None, "tok", "loop"),
        P(None, "tok", "loop"),
        P(None, "loop", "tok"),
        P("loop", "tok"),
    )
    return jax.shard_map(
        local,
        mesh=mesh,
        in_specs=placed,
        out_specs=(
            P("loop", "tok"),
            P("loop", "tok"),
            P(None, "tok", "loop"),
            P(None, "tok", "loop"),
            P(None, "loop", "tok"),
        ),
        check_vma=False,
    )
```

time: 460 us -> 173 us (0.38)
  waiting for transfers between devices: 388 us -> 0 us
  Pallas kernels: 0 us -> 167 us
  matrix products: 21.2 us -> 0.32 us
  other arithmetic: 17 us -> 2.86 us
  between operations: 14.2 us -> 0.71 us
  local copies, waits for them, and re-layouts: 12.7 us -> 1.58 us
  starting transfers between devices: 6.57 us -> 0 us
    all_gather x3 -> x0, waiting for transfers between devices: 208 us -> none  [the longest x1 76.8 us: local(): acts = lax.all_gather(jnp.stack(acts), 'tok', axis=0, tiled=False)]
    pallas_call x0 -> x2, Pallas kernels: none -> 167 us  [the longest x1 163 us: everything(): pl.pallas_call(kernel, out_shape=(jax.ShapeDtypeStruct((held, width), bf1...]
    reduce_scatter x1 -> x0, waiting for transfers between devices: 124 us -> none  [local(): lax.psum_scatter(jnp.concatenate([out_part, in_part], axis=1), 'loop', sc...]
    all_to_all x1 -> x0, waiting for transfers between devices: 55.8 us -> none  [local(): lax.all_to_all(hidden.astype(jnp.bfloat16), 'tok', 0, 0, tiled=True)]
    dot_general x22 -> x2, matrix products: 21.2 us -> 0.32 us  [mm(): lax.dot_general(a, b, (((ca,), (cb,)), ((), ())), preferred_element_type=...]
    slice x5 -> x0, local copies, waits for them, and re-layouts: 7.34 us -> none  [the longest x1 3.66 us: local(): everyone[:, e].reshape(loops * SLOTS, 2 * width)]
    all_to_all x1 -> x0, starting transfers between devices: 6.23 us -> none  [local(): lax.all_to_all(hidden.astype(jnp.bfloat16), 'tok', 0, 0, tiled=True)]
  transfers between devices with their start and end apart: 5 -> 0, of which waited for: 5 -> 0; matrix products, arithmetic and copies ran while one was open for 2% -> 0% of each run, Pallas kernels for 0% -> 0%
where the time goes in v4:
time: 173 us; the launch traced here: 172 us
  Pallas kernels  167 us (97%)
  other arithmetic  2.86 us (2%)
    pallas_call x1, Pallas kernels, everything(): pl.pallas_call(kernel, out_shape=(jax.ShapeDtypeStruct((held, width), bf1...  163 us
    pallas_call x1, Pallas kernels, hand_over(): pl.pallas_call(hand_over_kernel, out_shape=tuple((jax.ShapeDtypeStruct(a....  3.49 us

profile of v4, /device:TPU:1, one launch (start us, length us, event | category | flops | bytes accessed | tf_op | source)
XLA Modules:
  0.0 172.3 jit_solution(11021926761041698416)
XLA Ops:
  0.6 0.0 copy-start.2
  0.6 0.0 copy-start
  0.7 0.7 copy-done.2
  1.3 0.3 compare_reduce_fusion
  1.6 0.1 pad.2.clone
  1.7 0.1 eq.52
  1.8 0.1 convert_reduce_fusion
  1.9 0.1 select_reduce_fusion
  2.1 0.1 convert_reduce_fusion.1
  2.2 0.1 fusion
  2.3 1.4 maximum_maximum_fusion.lanes8
  3.7 0.0 copy-done
  3.7 0.0 copy-start.1
  3.7 0.2 convolution_convert_fusion
  3.8 0.7 copy-done.1
  4.6 0.2 convolution_convert_fusion.1
  4.7 0.7 pad_maximum_fusion.sent
  5.5 163.3 %everything.1 = (bf16[128,512]{1,0:T(8,128)(2,1)}, bf16[128,512]{1,0:T(8,128)(2,1)}, bf16[2,448,512]{2,1,0:T(8,128)(2,1)}, bf16[2,448,512]{2,1,0:T(8,128)(2,1)}, bf16[2,448,512]{2,1,0:T(8,128)(2,1)}) custom-call(bf16[2,2,48,512]{3,2,1,0:T(8,128)(2,1)} %pad_maximum_fusion.sent, f32[8,768]{1,0:T(8,128)} %maximum_maximum_fusion.lanes8, s32[2,768]{1,0:T(2,128)} %tokens.1, ...), custom_call_target="tpu_custom_call" | custom-call | tf_op jit(solution)/shard_map/everything/pallas_call | solution.py:585
  168.8 3.5 %hand_over.1 = (bf16[128,512]{1,0:T(8,128)(2,1)}, bf16[128,512]{1,0:T(8,128)(2,1)}, bf16[2,448,512]{2,1,0:T(8,128)(2,1)}, bf16[2,448,512]{2,1,0:T(8,128)(2,1)}, bf16[2,448,512]{2,1,0:T(8,128)(2,1)}) custom-call(bf16[128,512]{1,0:T(8,128)(2,1)} %get-tuple-element.15.refs_0_, bf16[128,512]{1,0:T(8,128)(2,1)} %get-tuple-element.16.refs_1_, ...), custom_call_target="tpu_custom_call" | custom-call | tf_op jit(solution)/shard_map/hand_over/pallas_call | solution.py:630
  (6 shorter events, 0.1 us)
Async XLA Ops:
  0.6 0.7 copy-start.2
  0.6 3.0 %copy-start = (bf16[128,512]{1,0:T(8,128)(2,1)S(1)}, bf16[128,512]{1,0:T(8,128)(2,1)}, u32[]{:S(2)}) copy-start(bf16[128,512]{1,0:T(8,128)(2,1)} %param.13) | copy-start | bytes 393220
  3.7 0.9 copy-start.1

commit v5 on v4

--- a/solution.py
+++ b/solution.py
@@ -76,7 +76,7 @@
                 self.add(chain, max(due, when))
 
 
-def kernel(sent, lanes8, tokens, gate_hbm, up_hbm, down_hbm, out_m, out_f, gate_g, up_g, down_g,
+def kernel(sent, place_of, weight_of, tokens, gate_hbm, up_hbm, down_hbm, out_m, out_f, gate_g, up_g, down_g,
            G, rows_of, part, post, mail, transit, landing, carry, sums, turn, acts, transit2,
            part2, total, box_p, box_q, crossing, joint, piece, everyone, staging, cols, gate_t, up_t, down_w, early,
            send_sems, recv_sems, own_sems, out_sems, in_sems):
@@ -304,40 +304,40 @@
         give(0)
         far(1)
         far(0)
-        yield T + f * 1.5
+        yield T + f[0] * 1.5
         give(1)
-        yield T + f * 2.8
+        yield T + f[0] * 2.8
         give(2)
-        yield T + f * 4.8
+        yield T + f[0] * 4.8
         pass_on(0)
-        yield T + f * 6.4
+        yield T + f[0] * 6.4
         near(1)
         near(0)
         give(3)
-        yield T + f * 7.9
+        yield T + f[1] * 7.9
         pass_on(1)
-        yield T + f * 8.5
+        yield T + f[1] * 8.5
         mix(0)
         far(2)
-        yield T + f * 10.0
+        yield T + f[1] * 10.0
         pass_on(2)
-        yield T + f * 12.0
+        yield T + f[1] * 12.0
         post[e, 4] = whole(1).astype(bf16)
         ferry.hop(4, post.at[e, 4])
         mix(1)
-        yield T + f * 13.0
+        yield T + f[1] * 13.0
         pass_on(3)
-        yield T + f * 14.0
+        yield T + f[1] * 14.0
         mix(2)
         near(2)
-        yield T + f * 16.0
+        yield T + f[1] * 16.0
         sums[e, pl.ds(0, p_rows)] = whole(0)
         pass_on(4)
-        yield T + f * 17.5
+        yield T + f[1] * 17.5
         mix(3)
-        yield T + f * 19.0
+        yield T + f[1] * 19.0
         sums[e, QR] = whole(2)
-        yield T + f * 20.0
+        yield T + f[1] * 20.0
         ferry.landed(4)
         sums[e, pl.ds(0, p_rows)] = sums[e, pl.ds(0, p_rows)] + landing[e, 4].astype(f32)
         settled(e)
@@ -377,41 +377,39 @@
         ring("q", turn.at[e, QR])
         ring("p", turn.at[e, PR])
         ferry.hop(1, turn.at[e, QR])
-        yield U + f * 4.0
+        yield U + f[0] * 4.0
         pass_on(0, 0, PR)
-        yield U + f * 4.6
+        yield U + f[0] * 4.6
         onward("q")
         ferry.hop(2, acts.at[tok_at(-1, high), e, QR])
         ferry.hop(3, acts.at[tok_at(1, high), e, QR])
-        yield U + f * 6.5
+        yield U + f[0] * 6.5
         pass_on(1, 0, QR)
-        yield U + f * 7.5
+        yield U + f[0] * 7.5
         ferry.landed(0)
         ring("m", acts.at[tok_at(0, far_high), e, PR])
         onward("p")
-        yield U + f * 8.5
+        yield U + f[0] * 8.5
         closed("q")
         ferry.hop(4, acts.at[tok_at(2, high), e, QR])
-        yield U + f * 9.5
+        yield U + f[0] * 9.5
         pass_on(2, -1, QR)
-        yield U + f * 12.0
+        yield U + f[0] * 12.0
         pass_on(3, 1, QR)
-        yield U + f * 13.0
+        yield U + f[0] * 13.0
         onward("m")
-        yield U + f * 14.5
+        yield U + f[0] * 14.5
         pass_on(4, 2, QR)
-        yield U + f * 16.0
+        yield U + f[1] * 16.0
         sender.all_landed(acts.at[pl.ds(0, 2), e, PR], ring_slot, to["y+"])
-        yield U + f * 18.0
+        yield U + f[1] * 16.2
         sender.all_landed(acts.at[pl.ds(0, 4), e, QR], last_slot, to["cross"])
         kept.wait()
 
     def product(e, z):
         scaled, gate_bar, up_bar = (acts[z, e, pl.ds(k * share, share)] for k in range(3))
-        part2[z, 0] = mm(scaled, down_w[e], 1, 0).reshape(part2.shape[2:])
-        part2[z, 1] = (mm(gate_bar, gate_t[e], 1, 0) + mm(up_bar, up_t[e], 1, 0)).reshape(part2.shape[2:])
-
-    last_offers, unsettled = [], set()
+        part2[e, z, 0] = mm(scaled, down_w[e], 1, 0).reshape(part2.shape[3:])
+        part2[e, z, 1] = (mm(gate_bar, gate_t[e], 1, 0) + mm(up_bar, up_t[e], 1, 0)).reshape(part2.shape[3:])
 
     def sum_loop(e, lanes, result, start, due):
         twins, crossed, run, ready = {}, {}, {}, set()
@@ -419,23 +417,14 @@
         p, q = lanes.get("P"), lanes.get("Q")
         kinds = (["own", "mate"] if p else []) + (["q"] if q else [])
         yield start
-        while unsettled:
-            start += 0.5
-            yield start
-        for copy in last_offers:
-            sender.gone(copy.number)
-        last_offers.clear()
-        unsettled.update(FAR_FIRST)
 
         def offer(d):
             product(e, spot(d))
-            twins[d] = sender.start(part2.at[spot(d), 1 - core], total.at[e, spot(d)], to["twin"])
-            last_offers.append(twins[d])
+            twins[d] = sender.start(part2.at[e, spot(d), 1 - core], total.at[e, spot(d)], to["twin"])
 
         def settle(d):
-            unsettled.remove(d)
             twins[d].wait_recv()
-            total[e, spot(d)] = total[e, spot(d)] + part2[spot(d), core]
+            total[e, spot(d)] = total[e, spot(d)] + part2[e, spot(d), core]
             if q:
                 crossed[d] = sender.start(
                     total.at[e, spot(d), far_side, q], crossing.at[e, FAR_FIRST.index(d), pl.ds(0, q.size)], to["low"])
@@ -526,20 +515,20 @@
         return spread_loop(lambda n: sent.at[e, n], lambda n, block: G.at[e, n, block], ("P", "Q"), due, G.at[e, 0])
 
     def chain(e):
-        start = (0.0, 12.0)[e]
-        yield from gather_in(e, tuple(start + t for t in ((3, 4, 8, 12, 16, 19, 21), (3, 7, 11, 15, 19.5, 23, 25))[e]))
+        start = (0.0, 8.0)[e]
+        yield from gather_in(e, tuple(start + t for t in ((3, 4, 8, 12, 16, 19, 21), (4, 8, 12, 16, 20, 24, 26))[e]))
         if e == 0:
             for load in loads:
                 load.wait()
-        yield from sum_tok(e, (22.0, 38.0)[e], (1.3, 1.6)[e])
-        yield from spread_tok(e, (50.0, 73.0)[e], 1.5)
+        yield from sum_tok(e, (22.0, 35.0)[e], ((1.3, 1.3), (1.32, 1.6))[e])
+        yield from spread_tok(e, (49.0, 69.0)[e], ((1.75, 1.91), (1.4, 1.53))[e])
         agenda.add(weight_grads(e), agenda.now + 3.0)
-        S = (80.0, 102.0)[e]
+        S = (80.5, 95.0)[e]
         yield from sum_loop(e, {"P": pl.ds(0, SLOTS // 2), "Q": pl.ds(SLOTS // 2, SLOTS // 2)}, e, S,
                             tuple(S + t for t in (3.5, 8.5, 13.5, 17.5, 20, 23)))
-        R = (106.0, 127.0)[e]
+        R = (103.6, 118.0)[e]
         yield from spread_loop(lambda n: piece.at[e], lambda n, block: everyone.at[e, block], ("PQ"[e],),
-                               tuple(R + t for t in ((4, 8, 12, 16, 20, 22, 24), (2.5, 4.5, 7, 9.5, 12, 13, 14))[e]),
+                               tuple(R + t for t in ((5.0, 9.0, 11.9, 17.0, 19.0, 21.5, 24.0), (2.5, 4.5, 7, 9.5, 12, 13, 14))[e]),
                                everyone.at[e, pl.ds(0, 16)])
         partial_result(e)
 
@@ -558,12 +547,13 @@
                 dst[...] = (early[k] + value).astype(bf16)
 
     def columns():
-        cols[...] = jnp.transpose(jnp.concatenate([lanes8[...], jnp.zeros((120, cols.shape[0]), f32)], axis=0))
+        cols[...] = jnp.transpose(jnp.concatenate(
+            [place_of[...].astype(f32), weight_of[...], jnp.zeros((124, cols.shape[0]), f32)], axis=0))
         yield
 
     agenda.add(chain(0), 0.0)
     agenda.add(columns(), 2.0)
-    agenda.add(chain(1), 12.0)
+    agenda.add(chain(1), 8.0)
     agenda.run()
 
     sender.drain()
@@ -571,9 +561,9 @@
         copy.wait()
 
 
-def everything(sent, lanes8, tokens, gate_t, up_t, down_w, held):
+def everything(sent, place, weight, tokens, gate_t, up_t, down_w, held):
     experts, panel, width = down_w.shape
-    total = lanes8.shape[1]
+    total = place.shape[1]
     toks = 8
     rows = 3 * total // toks
     p_rows = 160
@@ -585,7 +575,7 @@
     return pl.pallas_call(
         kernel,
         out_shape=(jax.ShapeDtypeStruct((held, width), bf16),) * 2 + (grads,) * 3,
-        in_specs=[VM] * 3 + [ANY] * 3,
+        in_specs=[VM] * 4 + [ANY] * 3,
         out_specs=(VM, VM, ANY, ANY, ANY),
         scratch_shapes=[
             V((experts, 2, 32, SLOTS, width), bf16),
@@ -600,7 +590,7 @@
             V((experts, rows, panel), bf16),
             V((toks, experts, rows, panel), bf16),
             V((experts, 5, 2, p_rows // 2, panel), bf16),
-            V((LAYERS, 2, 2, SLOTS, width), f32),
+            V((experts, LAYERS, 2, 2, SLOTS, width), f32),
             V((experts, LAYERS, 2, SLOTS, width), f32),
             V((experts, 2, 2, 4, SLOTS // 2, width), f32),
             V((experts, 2, 4, SLOTS // 2, width), f32),
@@ -617,7 +607,7 @@
         compiler_params=pltpu.CompilerParams(
             collective_id=0, has_side_effects=True, vmem_limit_bytes=67_043_328),
         name="everything",
-    )(sent, lanes8, tokens, gate_t, up_t, down_w)
+    )(sent, place, weight, tokens, gate_t, up_t, down_w)
 
 
 def hand_over_kernel(*refs):
@@ -647,7 +637,6 @@
     starts = jnp.sum((owner[:, None, :] < holder[None, :, None]).astype(jnp.int32), axis=2)
     start_of = jnp.sum(jnp.where(owner[:, :, None] == holder, starts[:, None, :], 0), axis=2)
     place = owner * SLOTS + jnp.arange(rows)[None, :] - start_of
-    lanes8 = jnp.concatenate([place.astype(jnp.float32), route_weight, jnp.zeros((4, rows), jnp.float32)], axis=0)
 
     own = jnp.arange(held) + me * held
     present = jnp.any(expert_rows[:, :, None] == own, axis=1)
@@ -659,7 +648,7 @@
         [mm(pick, v, 1, 0).astype(jnp.bfloat16).reshape(experts, SLOTS, width) for v in (features, out_grad)], axis=1
     )
     mixed, feature_grad, gate_grad, up_grad, down_grad = everything(
-        sent, lanes8, expert_rows, jnp.swapaxes(gate_proj, 1, 2), jnp.swapaxes(up_proj, 1, 2),
+        sent, place, route_weight, expert_rows, jnp.swapaxes(gate_proj, 1, 2), jnp.swapaxes(up_proj, 1, 2),
         down_proj, held)
     mixed, feature_grad, gate_grad, up_grad, down_grad = hand_over(mixed, feature_grad, gate_grad, up_grad, down_grad)
     return (mixed, feature_grad, jnp.swapaxes(gate_grad, 1, 2), jnp.swapaxes(up_grad, 1, 2), down_grad)

time: 173 us -> 161 us (0.931)
  Pallas kernels: 167 us -> 156 us
    pallas_call x1, Pallas kernels: 163 us -> 152 us  [everything(): pl.pallas_call(kernel, out_shape=(jax.ShapeDtypeStruct((held, width), bf1...]
where the time goes in v5:
time: 161 us
  Pallas kernels  156 us (97%)
  other arithmetic  2.07 us (1%)
    pallas_call x1, Pallas kernels, everything(): pl.pallas_call(kernel, out_shape=(jax.ShapeDtypeStruct((held, width), bf1...  152 us
    pallas_call x1, Pallas kernels, hand_over(): pl.pallas_call(hand_over_kernel, out_shape=tuple((jax.ShapeDtypeStruct(a....  3.49 us

profile of v5, /device:TPU:1, one launch (start us, length us, event | category | flops | bytes accessed | tf_op | source)
XLA Modules:
  0.0 160.7 jit_solution(18089823460499470304)
XLA Ops:
  0.6 0.0 copy-start.1
  0.7 0.7 copy-done.1
  1.3 0.3 compare_reduce_fusion
  1.6 0.1 eq.52
  1.7 0.1 convert_reduce_fusion
  1.9 0.1 select_reduce_fusion
  2.0 0.6 add_subtract_fusion.place_of
  2.6 0.1 convert_reduce_fusion.1
  2.7 0.0 copy-start
  2.7 0.1 fusion
  2.8 1.1 convolution_convert_fusion
  3.9 0.0 copy-done
  3.9 0.2 convolution_convert_fusion.1
  4.1 0.7 pad_maximum_fusion.sent
  4.8 152.5 %everything.1 = (bf16[128,512]{1,0:T(8,128)(2,1)}, bf16[128,512]{1,0:T(8,128)(2,1)}, bf16[2,448,512]{2,1,0:T(8,128)(2,1)}, bf16[2,448,512]{2,1,0:T(8,128)(2,1)}, bf16[2,448,512]{2,1,0:T(8,128)(2,1)}) custom-call(bf16[2,2,48,512]{3,2,1,0:T(8,128)(2,1)} %pad_maximum_fusion.sent, s32[2,768]{1,0:T(2,128)} %add_subtract_fusion.place_of, f32[2,768]{1,0:T(2,128)} %weight_of.1, ...), custom_call_target="tpu_custom_call" | custom-call | tf_op jit(solution)/shard_map/everything/pallas_call | solution.py:575
  157.2 3.5 %hand_over.1 = (bf16[128,512]{1,0:T(8,128)(2,1)}, bf16[128,512]{1,0:T(8,128)(2,1)}, bf16[2,448,512]{2,1,0:T(8,128)(2,1)}, bf16[2,448,512]{2,1,0:T(8,128)(2,1)}, bf16[2,448,512]{2,1,0:T(8,128)(2,1)}) custom-call(bf16[128,512]{1,0:T(8,128)(2,1)} %get-tuple-element.15.refs_0_, bf16[128,512]{1,0:T(8,128)(2,1)} %get-tuple-element.16.refs_1_, ...), custom_call_target="tpu_custom_call" | custom-call | tf_op jit(solution)/shard_map/hand_over/pallas_call | solution.py:620
  (4 shorter events, 0.0 us)
Async XLA Ops:
  0.6 0.7 copy-start.1
  2.7 1.2 copy-start

commit v6 on v5

--- a/solution.py
+++ b/solution.py
@@ -13,8 +13,8 @@
 SLOTS = 48
 LAYERS = 8
 FAR_FIRST = (4, 3, -3, 2, -2, 1, -1, 0)
-COPIES = 320
-RING = 64
+COPIES = 278
+RING = 32
 
 
 class Sender:
@@ -314,19 +314,19 @@
         near(1)
         near(0)
         give(3)
-        yield T + f[1] * 7.9
+        yield T + f[1] * 7.0
         pass_on(1)
-        yield T + f[1] * 8.5
+        yield T + f[1] * 7.3
         mix(0)
         far(2)
-        yield T + f[1] * 10.0
+        yield T + f[1] * 8.2
         pass_on(2)
+        yield T + f[1] * 10.8
+        pass_on(3)
         yield T + f[1] * 12.0
         post[e, 4] = whole(1).astype(bf16)
         ferry.hop(4, post.at[e, 4])
         mix(1)
-        yield T + f[1] * 13.0
-        pass_on(3)
         yield T + f[1] * 14.0
         mix(2)
         near(2)
@@ -520,12 +520,12 @@
         if e == 0:
             for load in loads:
                 load.wait()
-        yield from sum_tok(e, (22.0, 35.0)[e], ((1.3, 1.3), (1.32, 1.6))[e])
+        yield from sum_tok(e, (22.0, 35.0)[e], ((1.3, 1.37), (1.32, 1.6))[e])
         yield from spread_tok(e, (49.0, 69.0)[e], ((1.75, 1.91), (1.4, 1.53))[e])
         agenda.add(weight_grads(e), agenda.now + 3.0)
         S = (80.5, 95.0)[e]
         yield from sum_loop(e, {"P": pl.ds(0, SLOTS // 2), "Q": pl.ds(SLOTS // 2, SLOTS // 2)}, e, S,
-                            tuple(S + t for t in (3.5, 8.5, 13.5, 17.5, 20, 23)))
+                            tuple(S + t for t in ((5.6, 10.5, 14, 17.5, 20, 23.1), (3.5, 8.5, 13.5, 17.5, 20, 23))[e]))
         R = (103.6, 118.0)[e]
         yield from spread_loop(lambda n: piece.at[e], lambda n, block: everyone.at[e, block], ("PQ"[e],),
                                tuple(R + t for t in ((5.0, 9.0, 11.9, 17.0, 19.0, 21.5, 24.0), (2.5, 4.5, 7, 9.5, 12, 13, 14))[e]),

time: 161 us -> 160 us (level)
  no operation moved by 1% of the time
where the time goes in v6:
time: 160 us; the launch traced here: 159 us
  Pallas kernels  155 us (97%)
  other arithmetic  2.07 us (1%)
    pallas_call x1, Pallas kernels, everything(): pl.pallas_call(kernel, out_shape=(jax.ShapeDtypeStruct((held, width), bf1...  151 us
    pallas_call x1, Pallas kernels, hand_over(): pl.pallas_call(hand_over_kernel, out_shape=tuple((jax.ShapeDtypeStruct(a....  3.49 us

profile of v6, /device:TPU:1, one launch (start us, length us, event | category | flops | bytes accessed | tf_op | source)
XLA Modules:
  0.0 159.5 jit_solution(1366090803270376743)
XLA Ops:
  0.6 0.0 copy-start.1
  0.7 0.7 copy-done.1
  1.3 0.3 compare_reduce_fusion
  1.6 0.1 eq.52
  1.7 0.1 convert_reduce_fusion
  1.9 0.1 select_reduce_fusion
  2.0 0.6 add_subtract_fusion.place_of
  2.6 0.1 convert_reduce_fusion.1
  2.7 0.0 copy-start
  2.7 0.1 fusion
  2.8 1.1 convolution_convert_fusion
  3.9 0.0 copy-done
  3.9 0.2 convolution_convert_fusion.1
  4.1 0.7 pad_maximum_fusion.sent
  4.8 151.2 %everything.1 = (bf16[128,512]{1,0:T(8,128)(2,1)}, bf16[128,512]{1,0:T(8,128)(2,1)}, bf16[2,448,512]{2,1,0:T(8,128)(2,1)}, bf16[2,448,512]{2,1,0:T(8,128)(2,1)}, bf16[2,448,512]{2,1,0:T(8,128)(2,1)}) custom-call(bf16[2,2,48,512]{3,2,1,0:T(8,128)(2,1)} %pad_maximum_fusion.sent, s32[2,768]{1,0:T(2,128)} %add_subtract_fusion.place_of, f32[2,768]{1,0:T(2,128)} %weight_of.1, ...), custom_call_target="tpu_custom_call" | custom-call | tf_op jit(solution)/shard_map/everything/pallas_call | solution.py:575
  156.0 3.5 %hand_over.1 = (bf16[128,512]{1,0:T(8,128)(2,1)}, bf16[128,512]{1,0:T(8,128)(2,1)}, bf16[2,448,512]{2,1,0:T(8,128)(2,1)}, bf16[2,448,512]{2,1,0:T(8,128)(2,1)}, bf16[2,448,512]{2,1,0:T(8,128)(2,1)}) custom-call(bf16[128,512]{1,0:T(8,128)(2,1)} %get-tuple-element.15.refs_0_, bf16[128,512]{1,0:T(8,128)(2,1)} %get-tuple-element.16.refs_1_, ...), custom_call_target="tpu_custom_call" | custom-call | tf_op jit(solution)/shard_map/hand_over/pallas_call | solution.py:620
  (4 shorter events, 0.0 us)
Async XLA Ops:
  0.6 0.7 copy-start.1
  2.7 1.2 copy-start
